TPU v7x, 128 devices: a whole 4x4x4 slice. The times are simulated.
128 devices in a mesh: row: 4 (over y), col: 32 (over z, x, core).
Axes of the slice: x: 4, y: 4, z: 4, core: 2. Of those that a mesh axis runs over, the one named last changes fastest.
Arguments:
- dofs: float32 [504, 32768], P(None, ('row', 'col')), may hold values from -6 to 6
- star: float32 [243, 32768], P(None, ('row', 'col')), may hold values from -1.25 to 1.25
- flux_mats: float32 [648, 32768], P(None, ('row', 'col')), may hold values from -0.75 to 0.75
- kxi: float32 [3, 56, 56], replicated, may hold values from -0.75 to 0.75
- face_proj: float32 [4, 56, 21], replicated, may hold values from -0.75 to 0.75
- face_lift: float32 [4, 21, 56], replicated, may hold values from -1.25 to 1.25
- orient: float32 [3, 21, 21], replicated, may hold values from -1.25 to 1.25
- neighbour: int32 [4, 32768], P(None, ('row', 'col')), may hold values from 0 to 2047
- orient_code: int32 [4, 32768], P(None, ('row', 'col')), may hold values from 0 to 2
- send_list: int32 [4, 8192], P(None, ('row', 'col')), may hold values from 0 to 255
- fault_part: int32 [16384, 1], P(('row', 'col')), may hold values from 0 to 127; in each aligned block of 128 rows (0 to 127, 128 to 255, ...) at most 2 rows name the same one
- fault_item: int32 [16384], P(('row', 'col')), may hold values from 0 to 1023
- shear_init: float32 [21, 16384], P(None, ('row', 'col')), may hold values from -8 to 8
- normal_init: float32 [21, 16384], P(None, ('row', 'col')), may hold values from 1 to 8
- state_var: float32 [21, 16384], P(None, ('row', 'col')), may hold values from 0.3 to 0.7
- slip_prev: float32 [21, 16384], P(None, ('row', 'col')), may hold values from 0.05 to 2
Outputs:
- dofs_next: float32 [504, 32768], P(None, ('row', 'col'))
- slip_rate: float32 [21, 16384], P(None, ('row', 'col'))
Inputs may be any that keep to these rules, and one draw needn't show every extreme that they name: `fault_part`: partitions are numbered r * 32 + c. Among the 128 fault rows held by one device, no partition is named by more than 2 rows.
All inputs are finite; a program needn't handle non-finite values.
Results may differ from a plain program's by a relative error of at most 0.0003.
Values sent between devices are 32-bit elements; how exact they have to be, the bound alone decides.
A program may use at most 128 MiB of HBM per device.

v0:
```python
import jax
import jax.numpy as jnp
from jax import lax
from jax.experimental import pallas as pl
from jax.experimental.pallas import tpu as pltpu
from jax.sharding import PartitionSpec as P

QUANT = 9
BASIS = 56
FACE = 21
ORDER = 6
NEWTON_ITERS = 3
TIME_STEP = 2.0
FRIC_A = 0.5
MESH = pl.DeviceIdType.MESH
BF = jnp.bfloat16
F32 = jnp.float32

Q_ORDER = (0, 3, 6, 1, 2, 4, 5, 7, 8)
HEAD = 3 * 128


def iota(shape, dim):
    return lax.broadcasted_iota(jnp.int32, shape, dim)


def ones_at(mask):
    return jnp.where(mask, 1.0, 0.0).astype(BF)


def nn(a, b):
    return jnp.dot(a, b, preferred_element_type=F32)


def nt(a, b):
    return lax.dot_general(a, b, (((1,), (1,)), ((), ())), preferred_element_type=F32)


def split(x):
    high = x.astype(BF)
    return high, (x - high.astype(F32)).astype(BF)


def eye(rows, cols):
    return ones_at(iota((rows, cols), 0) == iota((rows, cols), 1))


def place(rows, cols, offsets):
    delta = iota((rows, cols), 1) - iota((rows, cols), 0)
    mask = delta == offsets[0]
    for offset in offsets[1:]:
        mask = mask | (delta == offset)
    return ones_at(mask)


def padded(x):
    return jnp.concatenate([x, jnp.zeros((8, x.shape[1]), F32)], axis=0)


def stacked(x):
    high, low = split(x)
    return jnp.concatenate([high, high, low], axis=0)


def inverse_sinh(value):
    magnitude = jnp.abs(value)
    squared = magnitude * magnitude
    positive = jnp.log1p(magnitude + squared / (1.0 + jnp.sqrt(1.0 + squared)))
    return jnp.where(value < 0.0, -positive, positive)


def friction_solve(shear, normal, shear_init, normal_init, state_var, slip_prev):
    shear_total = shear_init + shear
    normal_eff = normal_init * (1.0 + 0.5 * jnp.tanh(normal))
    growth = jnp.exp(state_var / FRIC_A) * 0.5
    slip_now = slip_prev
    for _ in range(NEWTON_ITERS):
        scaled = growth * slip_now
        misfit = shear_total - slip_now - FRIC_A * normal_eff * inverse_sinh(scaled)
        slope_val = -1.0 - FRIC_A * normal_eff * growth / jnp.sqrt(1.0 + scaled * scaled)
        slip_now = slip_now - misfit / slope_val
    return slip_now


def kernel(
    n_row, n_col,
    dofs, star, flux, kxi, proj, lift, orient, nbr, ocode, slist, fpart, fitem, sh0, nm0, stv, slp,
    out, slip_out,
    wk, wv, wp, wo, wl, adv, integ, ihl, xs, glb, gtab, nvals, comb, fvals, ohk, mpart,
    gsend, grecv, qsend, qrecv, asend, arecv, vsend, vrecv,
    gs_sem, gr_sem, q_sem, a_sem, v_sem, loc_sem,
):
    devices = n_row * n_col
    row, col = lax.axis_index("row"), lax.axis_index("col")
    me = row * n_col + col

    barrier = pltpu.get_barrier_semaphore()

    def partner(s):
        p = lax.rem(me + s, devices)
        return p, (p // n_col, lax.rem(p, n_col))

    def greet(s, _):
        _, where = partner(s)
        pl.semaphore_signal(barrier, inc=1, device_id=where, device_id_type=MESH)
        return 0

    lax.fori_loop(1, devices, greet, 0)

    def exchange_start(send, recv, sem, local_sem):
        def one(s, _):
            p, where = partner(s)
            pltpu.make_async_remote_copy(
                src_ref=send.at[pl.ds(p, 1)],
                dst_ref=recv.at[pl.ds(me, 1)],
                send_sem=sem.at[0],
                recv_sem=sem.at[1],
                device_id=where,
                device_id_type=MESH,
            ).start()
            return 0

        lax.fori_loop(1, devices, one, 0)
        pltpu.make_async_copy(send.at[pl.ds(me, 1)], recv.at[pl.ds(me, 1)], local_sem).start()

    def exchange_wait(send, recv, sem, local_sem):
        part = pl.ds(0, devices - 1)
        pltpu.make_async_copy(recv.at[part], recv.at[part], sem.at[1]).wait()
        pltpu.make_async_copy(send.at[pl.ds(me, 1)], recv.at[pl.ds(me, 1)], local_sem).wait()

    def exchange_end(send, sem):
        part = pl.ds(0, devices - 1)
        pltpu.make_async_copy(send.at[part], send.at[part], sem.at[0]).wait()

    at_high, at_low = place(BASIS, 192, (0, 128)), place(BASIS, 192, (64,))
    eye_b = eye(BASIS, BASIS)
    back, forth = [], []
    for d in range(3):
        high, low = split(kxi[d])
        forth.append(nn(high, at_high) + nn(low, at_low))
        back.append(nn(nt(eye_b, high).astype(BF), at_high) + nn(nt(eye_b, low).astype(BF), at_low))
    wk[...] = jnp.concatenate(back, axis=0).astype(BF)
    wv[...] = jnp.concatenate(forth, axis=0).astype(BF)
    rows = []
    pick_f = eye(32, FACE)
    for j in range(4):
        high, low = split(proj[j])
        rows.append(nn(nt(pick_f, high).astype(BF), at_high) + nn(nt(pick_f, low).astype(BF), at_low))
    wp[...] = jnp.concatenate(rows, axis=0).astype(BF)
    rows = []
    pick_g = eye(24, FACE)
    turn_high, turn_low = place(FACE, 96, (0, 64)), place(FACE, 96, (32,))
    for o in range(3):
        high, low = split(orient[o])
        rows.append(nn(nt(pick_g, high).astype(BF), turn_high) + nn(nt(pick_g, low).astype(BF), turn_low))
    wo[...] = jnp.concatenate(rows, axis=0).astype(BF)
    table = jnp.zeros((BASIS, 192), F32)
    for j in range(4):
        high, low = split(lift[j])
        table = table + nn(nt(eye_b, high).astype(BF), place(FACE, 192, (24 * j,)))
        table = table + nn(nt(eye_b, low).astype(BF), place(FACE, 192, (96 + 24 * j,)))
    wl[...] = table.astype(BF)

    square = (devices, fitem.shape[1])
    wide_part = jnp.broadcast_to(fpart[...], square)
    part_row = jnp.sum(jnp.where(iota(square, 0) == iota(square, 1), wide_part, 0), axis=0, keepdims=True)
    earlier = (wide_part == part_row) & (iota(square, 0) < iota(square, 1))
    rank_row = jnp.sum(jnp.where(earlier, 1, 0), axis=0, keepdims=True)
    names = iota(square, 0) == part_row
    mpart[0] = ones_at(names & (rank_row == 0))
    mpart[1] = ones_at(names & (rank_row == 1))
    code_row = (fitem[...] + 1).astype(F32)
    asked = [
        jnp.sum(jnp.where(names & (rank_row == k), code_row, 0.0), axis=1, keepdims=True) for k in range(2)
    ]
    low_lane = iota((devices, 128), 1) < 64
    qsend[...] = jnp.where(low_lane, asked[0], asked[1])

    def put(weights, value, target, q):
        target[q] = nn(weights[...], stacked(padded(value)))

    for q in range(QUANT):
        start = dofs[q * BASIS:(q + 1) * BASIS, :]
        integ[q] = TIME_STEP * start
        put(wk, start, adv.at[0], q)

    pl.semaphore_wait(barrier, devices - 1)
    exchange_start(qsend, qrecv, q_sem, loc_sem.at[0])

    def star_block(source, first):
        totals = [None] * 3
        for q in range(QUANT):
            for d in range(3):
                value = source[q, d * BASIS:(d + 1) * BASIS, :]
                for i in range(3):
                    r = (d * QUANT + first + i) * QUANT + q
                    term = star[r:r + 1, :] * value
                    totals[i] = term if totals[i] is None else totals[i] + term
        return totals

    factor = TIME_STEP
    for k in range(1, ORDER):
        factor = factor * TIME_STEP / (k + 1)
        source, target = adv.at[(k - 1) % 2], adv.at[k % 2]
        for first in range(0, QUANT, 3):
            for i, total in enumerate(star_block(source, first)):
                p = first + i
                if k < ORDER - 1:
                    integ[p] = integ[p] + factor * total
                    put(wk, total, target, p)
                else:
                    high, low = split(padded(integ[p] + factor * total))
                    block = Q_ORDER.index(p) * 128
                    ihl[block:block + 64, :] = high
                    ihl[block + 64:block + 128, :] = low
                    both = jnp.concatenate([high, high, low], axis=0)
                    target[p] = nn(wv[...], both)
                    xs[p] = nn(wp[...], both)
    turned = adv.at[(ORDER - 1) % 2]

    small = slist.shape[1]
    spread = ones_at(lax.rem(iota((small, 4 * small), 1), small) == iota((small, 4 * small), 0))
    listed = nn(slist[...].astype(F32).astype(BF), spread)
    listed = jnp.sum(
        jnp.where(iota((4, 4 * small), 1) // small == iota((4, 4 * small), 0), listed, 0.0), axis=0, keepdims=True
    ).astype(jnp.int32)
    elems = dofs.shape[1]
    picked = nn(ihl[...], ones_at(iota((elems, 4 * small), 0) == listed))
    half = iota((BASIS, 128), 1) < 64

    def pick(q, side):
        block = Q_ORDER.index(q) * 128
        lanes = slice(side * 128, side * 128 + 128)
        return picked[block:block + BASIS, lanes] + picked[block + 64:block + 64 + BASIS, lanes]

    for side in range(2):
        for q in range(5):
            first = pick(q, side)
            second = pick(q + 5, side) if q < 4 else first
            gsend[2 * side, q] = jnp.where(half, first, pltpu.roll(second, 64, 1))
            gsend[2 * side + 1, q] = jnp.where(half, pltpu.roll(first, 64, 1), second)
    targets = (
        (lax.rem(row + 1, n_row), col),
        (lax.rem(row + n_row - 1, n_row), col),
        (row, lax.rem(col + 1, n_col)),
        (row, lax.rem(col + n_col - 1, n_col)),
    )
    ghost_copies = [
        pltpu.make_async_remote_copy(
            src_ref=gsend.at[d],
            dst_ref=grecv.at[d],
            send_sem=gs_sem.at[d],
            recv_sem=gr_sem.at[d],
            device_id=targets[d],
            device_id_type=MESH,
        )
        for d in range(4)
    ]
    for copy in ghost_copies:
        copy.start()

    for first in range(0, QUANT, 3):
        for i, total in enumerate(star_block(turned, first)):
            p = first + i
            integ[p] = dofs[p * BASIS:(p + 1) * BASIS, :] + 0.25 * total

    def flux_block(j, side, first, read):
        totals = [None] * 3
        for q in range(QUANT):
            value = read(q)
            for i in range(3):
                r = ((j * 2 + side) * QUANT + first + i) * QUANT + q
                term = flux[r:r + 1, :] * value
                totals[i] = term if totals[i] is None else totals[i] + term
        return totals

    for j in range(4):
        for first in range(0, QUANT, 3):
            for i, total in enumerate(flux_block(j, 0, first, lambda q: xs[q, 32 * j:32 * j + 24, :])):
                comb[first + i, 24 * j:24 * j + 24, :] = total

    square_e = (elems, elems)
    for j in range(4):
        seen = nbr[j:j + 1, :]
        key = jnp.where(seen < 4 * elems, seen & (elems - 1), -1)
        glb[j] = nn(ihl[...], ones_at(iota(square_e, 0) == key)).astype(BF)

    exchange_wait(qsend, qrecv, q_sem, loc_sem.at[0])
    for k in range(2):
        item = qrecv[:, 64 * k:64 * k + 1].astype(jnp.int32) - 1
        ohk[k * devices:(k + 1) * devices, :] = ones_at(iota((devices, 4 * elems), 1) == item)

    inside = (row > 0, row < n_row - 1, col > 0, col < n_col - 1)
    for copy in ghost_copies:
        copy.wait_recv()
    for side in range(2):
        lanes = slice(side * 128, side * 128 + 128)
        for q in range(5):
            first = jnp.where(inside[2 * side], grecv[2 * side, q], 0.0)
            second = jnp.where(inside[2 * side + 1], grecv[2 * side + 1, q], 0.0)
            halves = [(q, jnp.where(half, first, pltpu.roll(second, 64, 1)))]
            if q < 4:
                halves.append((q + 5, jnp.where(half, pltpu.roll(first, 64, 1), second)))
            for quant, value in halves:
                high, low = split(padded(value))
                block = Q_ORDER.index(quant) * 128
                gtab[block:block + 64, lanes] = high
                gtab[block + 64:block + 128, lanes] = low

    def neighbours(j, start, stop):
        seen = nbr[j:j + 1, :]
        key = jnp.where(seen < 4 * elems, -1, seen & (elems - 1))
        face = lax.shift_right_logical(seen, 8) & 3
        code = ocode[j:j + 1, :]
        got = nn(gtab[start:stop, :], ones_at(iota(square_e, 0) == key)).astype(BF) + glb[j, start:stop, :]
        for block in range(start // 128, stop // 128):
            at = block * 128 - start
            high, low = got[at:at + 64], got[at + 64:at + 128]
            traces = nn(wp[...], jnp.concatenate([high, high, low], axis=0))
            value = traces[0:32]
            for f in range(1, 4):
                value = jnp.where(face == f, traces[32 * f:32 * f + 32], value)
            turns = nn(wo[...], stacked(value))
            value = turns[0:24]
            for o in range(1, 3):
                value = jnp.where(code == o, turns[24 * o:24 * o + 24], value)
            nvals[j, Q_ORDER[block]] = value

    fvals[...] = jnp.zeros_like(fvals)
    for j in range(4):
        neighbours(j, 0, HEAD)
        lanes = slice(j * elems, (j + 1) * elems)
        x0, x3, x6 = (xs[q, 32 * j:32 * j + 24, :] for q in (0, 3, 6))
        n0, n3, n6 = (nvals[j, q] for q in (0, 3, 6))
        fvals[0:24, lanes] = 0.5 * (x3 + n3) + 0.5 * (x6 - n6)
        fvals[24:48, lanes] = 0.5 * (x0 + n0)

    high, low = split(fvals[...])
    blank = jnp.zeros_like(high)
    answers = jnp.zeros((devices, 128), F32)
    for k in range(2):
        rows_k = ohk[k * devices:(k + 1) * devices, :]
        for part in (high, low):
            answers = answers + nt(rows_k, jnp.concatenate([part, blank] if k == 0 else [blank, part], axis=0))
    asend[...] = answers
    exchange_start(asend, arecv, a_sem, loc_sem.at[1])

    for j in range(4):
        neighbours(j, HEAD, 9 * 128)
    for j in range(4):
        for first in range(0, QUANT, 3):
            for i, total in enumerate(flux_block(j, 1, first, lambda q: nvals[j, q])):
                spot = (first + i, slice(24 * j, 24 * j + 24))
                comb[spot[0], spot[1], :] = comb[spot[0], spot[1], :] + total

    def lifted(value):
        high, low = split(value)
        return nn(wl[...], jnp.concatenate([high, high], axis=0)) + nn(wl[:, 0:96], low)

    for p in range(QUANT):
        out[p * BASIS:(p + 1) * BASIS, :] = integ[p] + 0.25 * lifted(comb[p])

    exchange_wait(asend, arecv, a_sem, loc_sem.at[1])
    high, low = split(arecv[...])
    eye_p = eye(128, 128)
    both = mpart[0] + mpart[1]
    own = nn(nt(eye_p, high).astype(BF), both) + nn(nt(eye_p, low).astype(BF), both)
    first_slot = rank_row == 0
    shear = jnp.where(first_slot, own[0:FACE], own[64:64 + FACE])
    normal = jnp.where(first_slot, own[24:24 + FACE], own[88:88 + FACE])
    slip = friction_solve(shear, normal, sh0[...], nm0[...], stv[...], slp[...])
    slip_out[...] = slip
    tall = jnp.concatenate([slip, jnp.zeros((64 - FACE, slip.shape[1]), F32)], axis=0)
    high, low = split(tall)
    blank = jnp.zeros_like(high)
    going = jnp.zeros((devices, 128), F32)
    for k in range(2):
        for part in (high, low):
            going = going + nt(mpart[k], jnp.concatenate([part, blank] if k == 0 else [blank, part], axis=0))
    vsend[...] = going
    exchange_start(vsend, vrecv, v_sem, loc_sem.at[2])

    exchange_wait(vsend, vrecv, v_sem, loc_sem.at[2])
    high, low = split(vrecv[...])
    rows = []
    for part in (high, low):
        sides = [
            nt(ones_at(iota((24, 128), 1) == iota((24, 128), 0) + 64 * k), part) for k in range(2)
        ]
        rows.append(jnp.concatenate(sides, axis=1))
    spread = nn(jnp.concatenate(rows, axis=0).astype(BF), ohk[...])
    spread = spread[0:24] + spread[24:48]
    push = lifted(jnp.concatenate([spread[:, j * elems:(j + 1) * elems] for j in range(4)], axis=0))
    out[3 * BASIS:4 * BASIS, :] = out[3 * BASIS:4 * BASIS, :] - 0.5 * push
    out[6 * BASIS:7 * BASIS, :] = out[6 * BASIS:7 * BASIS, :] + 0.5 * push

    for copy in ghost_copies:
        copy.wait_send()
    exchange_end(qsend, q_sem)
    exchange_end(asend, a_sem)
    exchange_end(vsend, v_sem)


def solution(mesh):
    n_row, n_col = mesh.shape["row"], mesh.shape["col"]
    devices = n_row * n_col

    def per_device(dofs, star, flux, kxi, proj, lift, orient, nbr, ocode, slist, fpart, fitem, sh0, nm0, stv, slp):
        elems = dofs.shape[1]
        vmem = pl.BlockSpec(memory_space=pltpu.VMEM)
        table = pltpu.VMEM((devices, 128), F32)
        pair = pltpu.SemaphoreType.DMA((2,))
        four = pltpu.SemaphoreType.DMA((4,))
        return pl.pallas_call(
            lambda *refs: kernel(n_row, n_col, *refs),
            out_shape=(
                jax.ShapeDtypeStruct(dofs.shape, F32),
                jax.ShapeDtypeStruct(slp.shape, F32),
            ),
            in_specs=[vmem] * 16,
            out_specs=(vmem, vmem),
            scratch_shapes=[
                pltpu.VMEM((3 * BASIS, 192), BF),
                pltpu.VMEM((3 * BASIS, 192), BF),
                pltpu.VMEM((128, 192), BF),
                pltpu.VMEM((72, 96), BF),
                pltpu.VMEM((BASIS, 192), BF),
                pltpu.VMEM((2, QUANT, 3 * BASIS, elems), F32),
                pltpu.VMEM((QUANT, BASIS, elems), F32),
                pltpu.VMEM((QUANT * 128, elems), BF),
                pltpu.VMEM((QUANT, 128, elems), F32),
                pltpu.VMEM((4, QUANT * 128, elems), BF),
                pltpu.VMEM((QUANT * 128, elems), BF),
                pltpu.VMEM((4, QUANT, 24, elems), F32),
                pltpu.VMEM((QUANT, 96, elems), F32),
                pltpu.VMEM((64, 4 * elems), F32),
                pltpu.VMEM((2 * devices, 4 * elems), BF),
                pltpu.VMEM((2, devices, 128), BF),
                pltpu.VMEM((4, 5, BASIS, 128), F32),
                pltpu.VMEM((4, 5, BASIS, 128), F32),
                table, table, table, table, table, table,
                four, four, pair, pair, pair, pltpu.SemaphoreType.DMA((3,)),
            ],
            compiler_params=pltpu.CompilerParams(collective_id=0, has_side_effects=True),
        )(dofs, star, flux, kxi, proj, lift, orient, nbr, ocode, slist, fpart, fitem.reshape(1, -1), sh0, nm0, stv, slp)

    split_cols = P(None, ("row", "col"))
    placed = (
        (split_cols,) * 3
        + (P(),) * 4
        + (split_cols,) * 3
        + (P(("row", "col"), None), P(("row", "col")))
        + (split_cols,) * 4
    )
    return jax.shard_map(
        per_device, mesh=mesh, in_specs=placed, out_specs=(split_cols, split_cols), check_vma=False
    )
```

profile of v0, /device:TPU:1, one launch (start us, length us, event | category | flops | bytes accessed | tf_op | source)
XLA Modules:
  0.0 52.6 jit_solution(4319744739054165533)
XLA Ops:
  0.6 0.0 copy-start.2
  0.6 1.4 %copy.19.refs_5_ = f32[4,21,56]{2,1,0:T(8,128)} copy(f32[4,21,56]{2,0,1:T(4,128)} %param.21) | data formatting | bytes 37632 | tf_op args[5]
  2.0 0.0 copy-done.2
  2.0 0.0 copy-start
  2.0 0.7 %copy.20.refs_10_ = s32[128,1]{1,0:T(8,128)} copy(s32[128,1]{0,1:T(1,128)S(1)} %copy-done.2) | data formatting | bytes 1024 | tf_op args[10]
  2.8 0.1 copy-done
  2.8 0.8 %copy.18.refs_4_ = f32[4,56,21]{2,1,0:T(8,128)} copy(f32[4,56,21]{1,0,2:T(4,128)S(1)} %copy-done) | data formatting | bytes 37632 | tf_op args[4]
  3.6 46.5 %shard_map.167 = (f32[504,256]{1,0:T(8,128)}, f32[21,128]{1,0:T(8,128)}) custom-call(f32[504,256]{1,0:T(8,128)} %refs_0_.1, f32[243,256]{1,0:T(8,128)} %refs_1_.1, f32[648,256]{1,0:T(8,128)} %refs_2_.1, f32[3,56,56]{2,1,0:T(8,128)} %refs_3_.1, f32[4,56,21]{2,1,0:T(8,128)} %copy.18.refs_4_, f32[4,21,56]{2,1,0:T(8,128)} %copy.19.refs_5_, ...), custom_call_target="tpu_custom_call" | custom-call | tf_op jit(solution)/shard_map/pallas_call | solution.py:414
  50.1 0.0 copy-start.1
  50.1 1.9 %copy.23 = f32[504,256]{1,0:T(8,128)} copy(f32[504,256]{1,0:T(8,128)} %get-tuple-element.4) | data formatting | bytes 1032192
  52.0 0.0 copy-done.1
  52.0 0.6 %copy.24 = f32[21,128]{1,0:T(8,128)} copy(f32[21,128]{1,0:T(8,128)S(1)} %copy-done.1) | data formatting | bytes 21504
Async XLA Ops:
  0.6 1.4 %copy-start.2 = (s32[128,1]{0,1:T(1,128)S(1)}, s32[128,1]{0,1:T(1,128)}, u32[]{:S(2)}) copy-start(s32[128,1]{0,1:T(1,128)} %param.26) | copy-start | bytes 1540
  2.0 0.8 %copy-start = (f32[4,56,21]{1,0,2:T(4,128)S(1)}, f32[4,56,21]{1,0,2:T(4,128)}, u32[]{:S(2)}) copy-start(f32[4,56,21]{1,0,2:T(4,128)} %param.20) | copy-start | bytes 56452
  50.1 1.9 %copy-start.1 = (f32[21,128]{1,0:T(8,128)S(1)}, f32[21,128]{1,0:T(8,128)}, u32[]{:S(2)}) copy-start(f32[21,128]{1,0:T(8,128)} %get-tuple-element.5) | copy-start | bytes 32260
where the time goes:
time: 52.9 us; the launch traced here: 52.6 us
  Pallas kernels  46.5 us (88%)
  local copies, waits for them, and re-layouts  5.42 us (10%)
  between operations  0.66 us (1%)
    pallas_call x1, Pallas kernels, per_device(): pl.pallas_call(lambda *refs: kernel(n_row, n_col, *refs), out_shape=(jax....  46.5 us
    unnamed x11, local copies, waits for them, and re-layouts  5.42 us

commit v1 on v0

--- a/solution.py
+++ b/solution.py
@@ -13,6 +13,7 @@
 TIME_STEP = 2.0
 FRIC_A = 0.5
 MESH = pl.DeviceIdType.MESH
+LOGICAL = pl.DeviceIdType.LOGICAL
 BF = jnp.bfloat16
 F32 = jnp.float32
 
@@ -86,7 +87,7 @@
     n_row, n_col,
     dofs, star, flux, kxi, proj, lift, orient, nbr, ocode, slist, fpart, fitem, sh0, nm0, stv, slp,
     out, slip_out,
-    wk, wv, wp, wo, wl, adv, integ, ihl, xs, glb, gtab, nvals, comb, fvals, ohk, mpart,
+    wk, wv, wp, wo, w12, tall, wl, adv, integ, ihl, xs, glb, gtab, nvals, comb, fvals, ohk, mpart,
     gsend, grecv, qsend, qrecv, asend, arecv, vsend, vrecv,
     gs_sem, gr_sem, q_sem, a_sem, v_sem, loc_sem,
 ):
@@ -96,31 +97,34 @@
 
     barrier = pltpu.get_barrier_semaphore()
 
-    def partner(s):
-        p = lax.rem(me + s, devices)
-        return p, (p // n_col, lax.rem(p, n_col))
-
-    def greet(s, _):
-        _, where = partner(s)
-        pl.semaphore_signal(barrier, inc=1, device_id=where, device_id_type=MESH)
-        return 0
-
-    lax.fori_loop(1, devices, greet, 0)
+    def ring(at, size, scale):
+        return [lax.rem(at + step, size) * scale for step in range(size)]
+
+    across = ring(row, n_row, n_col)
+    deep = ring(col // 8, 4, 8)
+    wide = ring(lax.rem(col, 8) // 2, 4, 2)
+    core = ring(lax.rem(col, 2), 2, 1)
+    hops = (0, 1, 2, 1)
+    steps = [(y, z, x, c) for y in range(4) for z in range(4) for x in range(4) for c in range(2)][1:]
+    steps.sort(key=lambda at: -(hops[at[0]] + hops[at[1]] + hops[at[2]]))
+
+    def partner(at):
+        return (across[at[0]] + deep[at[1]]) + (wide[at[2]] + core[at[3]])
+
+    for at in steps:
+        pl.semaphore_signal(barrier, inc=1, device_id=partner(at), device_id_type=LOGICAL)
 
     def exchange_start(send, recv, sem, local_sem):
-        def one(s, _):
-            p, where = partner(s)
+        for at in steps:
+            p = partner(at)
             pltpu.make_async_remote_copy(
                 src_ref=send.at[pl.ds(p, 1)],
                 dst_ref=recv.at[pl.ds(me, 1)],
                 send_sem=sem.at[0],
                 recv_sem=sem.at[1],
-                device_id=where,
-                device_id_type=MESH,
+                device_id=p,
+                device_id_type=LOGICAL,
             ).start()
-            return 0
-
-        lax.fori_loop(1, devices, one, 0)
         pltpu.make_async_copy(send.at[pl.ds(me, 1)], recv.at[pl.ds(me, 1)], local_sem).start()
 
     def exchange_wait(send, recv, sem, local_sem):
@@ -141,29 +145,38 @@
         back.append(nn(nt(eye_b, high).astype(BF), at_high) + nn(nt(eye_b, low).astype(BF), at_low))
     wk[...] = jnp.concatenate(back, axis=0).astype(BF)
     wv[...] = jnp.concatenate(forth, axis=0).astype(BF)
-    rows = []
-    pick_f = eye(32, FACE)
-    for j in range(4):
-        high, low = split(proj[j])
-        rows.append(nn(nt(pick_f, high).astype(BF), at_high) + nn(nt(pick_f, low).astype(BF), at_low))
-    wp[...] = jnp.concatenate(rows, axis=0).astype(BF)
+    flat = 4 * FACE
+    for g in range(FACE):
+        tall[0, 4 * g:4 * g + 4, :] = proj[g]
+        tall[1, 4 * g:4 * g + 4, :] = lift[g]
+    shape = (128, flat)
+    order = ones_at((iota(shape, 0) // 32 + 4 * lax.rem(iota(shape, 0), 32)) == iota(shape, 1))
+    high, low = split(tall[0])
+    proj_high, proj_low = nn(order, high).astype(BF), nn(order, low).astype(BF)
+    wp[...] = (nn(proj_high, at_high) + nn(proj_low, at_low)).astype(BF)
     rows = []
     pick_g = eye(24, FACE)
     turn_high, turn_low = place(FACE, 96, (0, 64)), place(FACE, 96, (32,))
     for o in range(3):
         high, low = split(orient[o])
         rows.append(nn(nt(pick_g, high).astype(BF), turn_high) + nn(nt(pick_g, low).astype(BF), turn_low))
-    wo[...] = jnp.concatenate(rows, axis=0).astype(BF)
-    table = jnp.zeros((BASIS, 192), F32)
-    for j in range(4):
-        high, low = split(lift[j])
-        table = table + nn(nt(eye_b, high).astype(BF), place(FACE, 192, (24 * j,)))
-        table = table + nn(nt(eye_b, low).astype(BF), place(FACE, 192, (96 + 24 * j,)))
+    turn = jnp.concatenate(rows, axis=0).astype(BF)
+    for j in range(4):
+        own_rows = slice(32 * j, 32 * j + 32)
+        both = jnp.concatenate([proj_high[own_rows], proj_high[own_rows], proj_low[own_rows]], axis=0)
+        high, low = split(nn(turn, both))
+        wo[72 * j:72 * j + 72, :] = nn(high, at_high) + nn(low, at_low)
+    w12[...] = wo[...].astype(BF)
+    shape = (flat, 192)
+    spot = 24 * lax.rem(iota(shape, 0), 4) + iota(shape, 0) // 4
+    high, low = split(tall[1])
+    table = nn(nt(eye_b, high).astype(BF), ones_at(iota(shape, 1) == spot))
+    table = table + nn(nt(eye_b, low).astype(BF), ones_at(iota(shape, 1) == spot + 96))
     wl[...] = table.astype(BF)
 
     square = (devices, fitem.shape[1])
-    wide_part = jnp.broadcast_to(fpart[...], square)
-    part_row = jnp.sum(jnp.where(iota(square, 0) == iota(square, 1), wide_part, 0), axis=0, keepdims=True)
+    part_row = fpart[...]
+    wide_part = jnp.sum(jnp.where(iota(square, 0) == iota(square, 1), part_row, 0), axis=1, keepdims=True)
     earlier = (wide_part == part_row) & (iota(square, 0) < iota(square, 1))
     rank_row = jnp.sum(jnp.where(earlier, 1, 0), axis=0, keepdims=True)
     names = iota(square, 0) == part_row
@@ -184,22 +197,25 @@
         integ[q] = TIME_STEP * start
         put(wk, start, adv.at[0], q)
 
-    pl.semaphore_wait(barrier, devices - 1)
-    exchange_start(qsend, qrecv, q_sem, loc_sem.at[0])
-
     def star_block(source, first):
-        totals = [None] * 3
-        for q in range(QUANT):
-            for d in range(3):
-                value = source[q, d * BASIS:(d + 1) * BASIS, :]
-                for i in range(3):
-                    r = (d * QUANT + first + i) * QUANT + q
-                    term = star[r:r + 1, :] * value
-                    totals[i] = term if totals[i] is None else totals[i] + term
-        return totals
+        sides = []
+        for lanes in (slice(0, 128), slice(128, 256)):
+            totals = [None] * 3
+            for q in range(QUANT):
+                for d in range(3):
+                    value = source[q, d * BASIS:(d + 1) * BASIS, lanes]
+                    for i in range(3):
+                        r = (d * QUANT + first + i) * QUANT + q
+                        term = star[r:r + 1, lanes] * value
+                        totals[i] = term if totals[i] is None else totals[i] + term
+            sides.append(totals)
+        return [jnp.concatenate([left, right], axis=1) for left, right in zip(*sides)]
 
     factor = TIME_STEP
     for k in range(1, ORDER):
+        if k == 3:
+            pl.semaphore_wait(barrier, devices - 1)
+            exchange_start(qsend, qrecv, q_sem, loc_sem.at[0])
         factor = factor * TIME_STEP / (k + 1)
         source, target = adv.at[(k - 1) % 2], adv.at[k % 2]
         for first in range(0, QUANT, 3):
@@ -310,20 +326,15 @@
     def neighbours(j, start, stop):
         seen = nbr[j:j + 1, :]
         key = jnp.where(seen < 4 * elems, -1, seen & (elems - 1))
-        face = lax.shift_right_logical(seen, 8) & 3
-        code = ocode[j:j + 1, :]
+        code = 3 * (lax.shift_right_logical(seen, 8) & 3) + ocode[j:j + 1, :]
         got = nn(gtab[start:stop, :], ones_at(iota(square_e, 0) == key)).astype(BF) + glb[j, start:stop, :]
         for block in range(start // 128, stop // 128):
             at = block * 128 - start
             high, low = got[at:at + 64], got[at + 64:at + 128]
-            traces = nn(wp[...], jnp.concatenate([high, high, low], axis=0))
-            value = traces[0:32]
-            for f in range(1, 4):
-                value = jnp.where(face == f, traces[32 * f:32 * f + 32], value)
-            turns = nn(wo[...], stacked(value))
+            turns = nn(w12[...], jnp.concatenate([high, high, low], axis=0))
             value = turns[0:24]
-            for o in range(1, 3):
-                value = jnp.where(code == o, turns[24 * o:24 * o + 24], value)
+            for c in range(1, 12):
+                value = jnp.where(code == c, turns[24 * c:24 * c + 24], value)
             nvals[j, Q_ORDER[block]] = value
 
     fvals[...] = jnp.zeros_like(fvals)
@@ -370,8 +381,8 @@
     normal = jnp.where(first_slot, own[24:24 + FACE], own[88:88 + FACE])
     slip = friction_solve(shear, normal, sh0[...], nm0[...], stv[...], slp[...])
     slip_out[...] = slip
-    tall = jnp.concatenate([slip, jnp.zeros((64 - FACE, slip.shape[1]), F32)], axis=0)
-    high, low = split(tall)
+    column = jnp.concatenate([slip, jnp.zeros((64 - FACE, slip.shape[1]), F32)], axis=0)
+    high, low = split(column)
     blank = jnp.zeros_like(high)
     going = jnp.zeros((devices, 128), F32)
     for k in range(2):
@@ -423,7 +434,9 @@
                 pltpu.VMEM((3 * BASIS, 192), BF),
                 pltpu.VMEM((3 * BASIS, 192), BF),
                 pltpu.VMEM((128, 192), BF),
-                pltpu.VMEM((72, 96), BF),
+                pltpu.VMEM((288, 192), F32),
+                pltpu.VMEM((288, 192), BF),
+                pltpu.VMEM((2, 4 * FACE, BASIS), F32),
                 pltpu.VMEM((BASIS, 192), BF),
                 pltpu.VMEM((2, QUANT, 3 * BASIS, elems), F32),
                 pltpu.VMEM((QUANT, BASIS, elems), F32),
@@ -442,7 +455,10 @@
                 four, four, pair, pair, pair, pltpu.SemaphoreType.DMA((3,)),
             ],
             compiler_params=pltpu.CompilerParams(collective_id=0, has_side_effects=True),
-        )(dofs, star, flux, kxi, proj, lift, orient, nbr, ocode, slist, fpart, fitem.reshape(1, -1), sh0, nm0, stv, slp)
+        )(
+            dofs, star, flux, kxi, jnp.transpose(proj, (2, 0, 1)), jnp.transpose(lift, (1, 0, 2)), orient,
+            nbr, ocode, slist, fpart.reshape(1, -1), fitem.reshape(1, -1), sh0, nm0, stv, slp,
+        )
 
     split_cols = P(None, ("row", "col"))
     placed = (

time: 52.9 us -> 42.1 us (0.80)
  Pallas kernels: 46.5 us -> 38.8 us
  local copies, waits for them, and re-layouts: 5.42 us -> 2.47 us
    pallas_call x1, Pallas kernels: 46.5 us -> 38.8 us  [per_device(): pl.pallas_call(lambda *refs: kernel(n_row, n_col, *refs), out_shape=(jax....]
    unnamed x11 -> x4, local copies, waits for them, and re-layouts: 5.42 us -> 2.47 us
where the time goes in v1:
time: 42.1 us; the launch traced here: 42 us
  Pallas kernels  38.8 us (92%)
  local copies, waits for them, and re-layouts  2.47 us (6%)
  between operations  0.65 us (2%)
    pallas_call x1, Pallas kernels, per_device(): pl.pallas_call(lambda *refs: kernel(n_row, n_col, *refs), out_shape=(jax....  38.8 us
    unnamed x4, local copies, waits for them, and re-layouts  2.47 us

profile of v1, /device:TPU:1, one launch (start us, length us, event | category | flops | bytes accessed | tf_op | source)
XLA Modules:
  0.0 42.0 jit_solution(8140774081133816936)
XLA Ops:
  0.6 38.8 %shard_map.167 = (f32[504,256]{1,0:T(8,128)}, f32[21,128]{1,0:T(8,128)}) custom-call(f32[504,256]{1,0:T(8,128)} %refs_0_.1, f32[243,256]{1,0:T(8,128)} %refs_1_.1, f32[648,256]{1,0:T(8,128)} %refs_2_.1, f32[3,56,56]{2,1,0:T(8,128)} %refs_3_.1, f32[21,4,56]{2,1,0:T(4,128)} %bitcast.4, f32[21,4,56]{2,1,0:T(4,128)} %bitcast.5, f32[3,21,21]{2,1,0:T(8,128)} %refs_6_.1, ...), custom_call_target="tpu_custom_call" | custom-call | tf_op jit(solution)/shard_map/pallas_call | solution.py:425
  39.5 0.0 copy-start
  39.5 1.9 %copy.20 = f32[504,256]{1,0:T(8,128)} copy(f32[504,256]{1,0:T(8,128)} %get-tuple-element.4) | data formatting | bytes 1032192
  41.4 0.0 copy-done
  41.4 0.6 %copy.21 = f32[21,128]{1,0:T(8,128)} copy(f32[21,128]{1,0:T(8,128)S(1)} %copy-done) | data formatting | bytes 21504
Async XLA Ops:
  39.5 1.9 %copy-start = (f32[21,128]{1,0:T(8,128)S(1)}, f32[21,128]{1,0:T(8,128)}, u32[]{:S(2)}) copy-start(f32[21,128]{1,0:T(8,128)} %get-tuple-element.5) | copy-start | bytes 32260

commit v2 on v1

v2 whole, which is shorter than its diff:
```python
import jax
import jax.numpy as jnp
from jax import lax
from jax.experimental import pallas as pl
from jax.experimental.pallas import tpu as pltpu
from jax.sharding import PartitionSpec as P

QUANT = 9
BASIS = 56
FACE = 21
ORDER = 6
NEWTON_ITERS = 3
TIME_STEP = 2.0
FRIC_A = 0.5
MESH = pl.DeviceIdType.MESH
LOGICAL = pl.DeviceIdType.LOGICAL
BF = jnp.bfloat16
F32 = jnp.float32

Q_ORDER = (0, 3, 6, 1, 2, 4, 5, 7, 8)
GROUPS = (Q_ORDER[0:3], Q_ORDER[3:6], Q_ORDER[6:9])
HEAD = 3 * 128
HEAD_PAIRS = ((0, 3), (6, 6))
REST_PAIRS = ((1, 2), (4, 5), (7, 8))
AT_SHEAR, AT_NORMAL, AT_STATE, AT_SLIP, AT_ITEM = 0, 24, 48, 72, 96


def iota(shape, dim):
    return lax.broadcasted_iota(jnp.int32, shape, dim)


def ones_at(mask):
    return jnp.where(mask, 1.0, 0.0).astype(BF)


def nn(a, b):
    return jnp.dot(a, b, preferred_element_type=F32)


def nt(a, b):
    return lax.dot_general(a, b, (((1,), (1,)), ((), ())), preferred_element_type=F32)


def split(x):
    high = x.astype(BF)
    return high, (x - high.astype(F32)).astype(BF)


def eye(rows, cols):
    return ones_at(iota((rows, cols), 0) == iota((rows, cols), 1))


def place(rows, cols, offsets):
    delta = iota((rows, cols), 1) - iota((rows, cols), 0)
    mask = delta == offsets[0]
    for offset in offsets[1:]:
        mask = mask | (delta == offset)
    return ones_at(mask)


def padded(x):
    return jnp.concatenate([x, jnp.zeros((8, x.shape[1]), F32)], axis=0)


def stacked(x):
    high, low = split(x)
    return jnp.concatenate([high, high, low], axis=0)


def inverse_sinh(value):
    magnitude = jnp.abs(value)
    squared = magnitude * magnitude
    positive = jnp.log1p(magnitude + squared / (1.0 + jnp.sqrt(1.0 + squared)))
    return jnp.where(value < 0.0, -positive, positive)


def friction_solve(shear, normal, shear_init, normal_init, state_var, slip_prev):
    shear_total = shear_init + shear
    normal_eff = normal_init * (1.0 + 0.5 * jnp.tanh(normal))
    growth = jnp.exp(state_var / FRIC_A) * 0.5
    slip_now = slip_prev
    for _ in range(NEWTON_ITERS):
        scaled = growth * slip_now
        misfit = shear_total - slip_now - FRIC_A * normal_eff * inverse_sinh(scaled)
        slope_val = -1.0 - FRIC_A * normal_eff * growth / jnp.sqrt(1.0 + scaled * scaled)
        slip_now = slip_now - misfit / slope_val
    return slip_now


def kernel(
    n_row, n_col,
    dofs_in, star_in, flux_in, kxi, proj, lift, orient, nbr, ocode, slist, fpart, fitem, sh0, nm0, stv, slp,
    out, slip_out,
    dofs, star, flux, result,
    wk, wv, wp, wo, w12, tall, wl, adv, integ, ihl, xs, glb, gtab, nvals, comb, fvals, oht, params,
    gsend, grecv, hsend, hrecv, qsend, qrecv, vsend, vrecv,
    gs_sem, gr_sem, hs_sem, hr_sem, q_sem, v_sem, loc_sem, in_sem, out_sem,
):
    devices = n_row * n_col
    loads = [
        pltpu.make_async_copy(source, target, in_sem.at[n])
        for n, (source, target) in enumerate(((dofs_in, dofs), (star_in, star), (flux_in, flux)))
    ]
    for load in loads:
        load.start()
    row, col = lax.axis_index("row"), lax.axis_index("col")
    me = row * n_col + col

    barrier = pltpu.get_barrier_semaphore()

    def ring(at, size, scale):
        return [lax.rem(at + step, size) * scale for step in range(size)]

    across = ring(row, n_row, n_col)
    deep = ring(col // 8, 4, 8)
    wide = ring(lax.rem(col, 8) // 2, 4, 2)
    core = ring(lax.rem(col, 2), 2, 1)
    hops = (0, 1, 2, 1)
    steps = [(y, z, x, c) for y in range(4) for z in range(4) for x in range(4) for c in range(2)][1:]
    steps.sort(key=lambda at: -(hops[at[0]] + hops[at[1]] + hops[at[2]]))

    def partner(at):
        return (across[at[0]] + deep[at[1]]) + (wide[at[2]] + core[at[3]])

    for at in steps:
        pl.semaphore_signal(barrier, inc=1, device_id=partner(at), device_id_type=LOGICAL)

    def own_copy(n, send, recv, local_sem):
        mine = pl.ds(n * me, n)
        return pltpu.make_async_copy(send.at[mine], recv.at[mine], local_sem)

    def exchange_start(n, send, recv, sem, local_sem):
        for at in steps:
            p = partner(at)
            pltpu.make_async_remote_copy(
                src_ref=send.at[pl.ds(n * p, n)],
                dst_ref=recv.at[pl.ds(n * me, n)],
                send_sem=sem.at[0],
                recv_sem=sem.at[1],
                device_id=p,
                device_id_type=LOGICAL,
            ).start()
        own_copy(n, send, recv, local_sem).start()

    def exchange_wait(n, send, recv, sem, local_sem):
        part = pl.ds(0, n * (devices - 1))
        pltpu.make_async_copy(recv.at[part], recv.at[part], sem.at[1]).wait()
        own_copy(n, send, recv, local_sem).wait()

    def exchange_end(n, send, sem):
        part = pl.ds(0, n * (devices - 1))
        pltpu.make_async_copy(send.at[part], send.at[part], sem.at[0]).wait()

    at_high, at_low = place(BASIS, 192, (0, 128)), place(BASIS, 192, (64,))
    eye_b = eye(BASIS, BASIS)
    back, forth = [], []
    for d in range(3):
        high, low = split(kxi[d])
        forth.append(nn(high, at_high) + nn(low, at_low))
        back.append(nn(nt(eye_b, high).astype(BF), at_high) + nn(nt(eye_b, low).astype(BF), at_low))
    wk[...] = jnp.concatenate(back, axis=0).astype(BF)
    wv[...] = jnp.concatenate(forth, axis=0).astype(BF)
    flat = 4 * FACE
    for g in range(FACE):
        tall[0, 4 * g:4 * g + 4, :] = proj[g]
        tall[1, 4 * g:4 * g + 4, :] = lift[g]
    shape = (128, flat)
    order = ones_at((iota(shape, 0) // 32 + 4 * lax.rem(iota(shape, 0), 32)) == iota(shape, 1))
    high, low = split(tall[0])
    proj_high, proj_low = nn(order, high).astype(BF), nn(order, low).astype(BF)
    wp[...] = (nn(proj_high, at_high) + nn(proj_low, at_low)).astype(BF)
    rows = []
    pick_g = eye(24, FACE)
    turn_high, turn_low = place(FACE, 96, (0, 64)), place(FACE, 96, (32,))
    for o in range(3):
        high, low = split(orient[o])
        rows.append(nn(nt(pick_g, high).astype(BF), turn_high) + nn(nt(pick_g, low).astype(BF), turn_low))
    turn = jnp.concatenate(rows, axis=0).astype(BF)
    for j in range(4):
        own_rows = slice(32 * j, 32 * j + 32)
        both = jnp.concatenate([proj_high[own_rows], proj_high[own_rows], proj_low[own_rows]], axis=0)
        high, low = split(nn(turn, both))
        wo[72 * j:72 * j + 72, :] = nn(high, at_high) + nn(low, at_low)
    w12[...] = wo[...].astype(BF)
    shape = (flat, 192)
    spot = 24 * lax.rem(iota(shape, 0), 4) + iota(shape, 0) // 4
    high, low = split(tall[1])
    table = nn(nt(eye_b, high).astype(BF), ones_at(iota(shape, 1) == spot))
    table = table + nn(nt(eye_b, low).astype(BF), ones_at(iota(shape, 1) == spot + 96))
    wl[...] = table.astype(BF)

    square = (devices, fitem.shape[1])
    part_row = fpart[...]
    wide_part = jnp.sum(jnp.where(iota(square, 0) == iota(square, 1), part_row, 0), axis=1, keepdims=True)
    earlier = (wide_part == part_row) & (iota(square, 0) < iota(square, 1))
    rank_row = jnp.sum(jnp.where(earlier, 1, 0), axis=0, keepdims=True)
    tall_square = (2 * devices, fitem.shape[1])
    slot_of = ones_at(iota(tall_square, 0) == 2 * part_row + rank_row)
    params[...] = jnp.zeros_like(params)
    for at, table in ((AT_SHEAR, sh0), (AT_NORMAL, nm0), (AT_STATE, stv), (AT_SLIP, slp)):
        params[at:at + FACE, :] = table[...]
    params[AT_ITEM:AT_ITEM + 1, :] = (fitem[...] + 1).astype(F32)
    high, low = split(params[...])
    qsend[...] = nt(slot_of, high) + nt(slot_of, low)

    def put(weights, value, target, q):
        target[q] = nn(weights[...], stacked(padded(value)))

    loads[0].wait()
    loads[1].wait()
    for q in Q_ORDER:
        start = dofs[q * BASIS:(q + 1) * BASIS, :]
        integ[q] = TIME_STEP * start
        put(wk, start, adv.at[0], q)

    def star_block(source, group):
        sides = []
        for lanes in (slice(0, 128), slice(128, 256)):
            totals = [None] * 3
            for q in Q_ORDER:
                for d in range(3):
                    value = source[q, d * BASIS:(d + 1) * BASIS, lanes]
                    for i, p in enumerate(group):
                        r = (d * QUANT + p) * QUANT + q
                        term = star[r:r + 1, lanes] * value
                        totals[i] = term if totals[i] is None else totals[i] + term
            sides.append(totals)
        return [(p, jnp.concatenate([left, right], axis=1)) for p, left, right in zip(group, *sides)]

    factor = TIME_STEP
    for k in range(1, ORDER - 1):
        if k == 3:
            pl.semaphore_wait(barrier, devices - 1)
            exchange_start(2, qsend, qrecv, q_sem, loc_sem.at[0])
        factor = factor * TIME_STEP / (k + 1)
        source, target = adv.at[(k - 1) % 2], adv.at[k % 2]
        for group in GROUPS:
            for p, total in star_block(source, group):
                integ[p] = integ[p] + factor * total
                put(wk, total, target, p)
    factor = factor * TIME_STEP / ORDER
    source, turned = adv.at[(ORDER - 2) % 2], adv.at[(ORDER - 1) % 2]

    small = slist.shape[1]
    elems = dofs.shape[1]
    spread = ones_at(lax.rem(iota((small, 4 * small), 1), small) == iota((small, 4 * small), 0))
    listed = nn(slist[...].astype(F32).astype(BF), spread)
    listed = jnp.sum(
        jnp.where(iota((4, 4 * small), 1) // small == iota((4, 4 * small), 0), listed, 0.0), axis=0, keepdims=True
    ).astype(jnp.int32)
    half = iota((BASIS, 128), 1) < 64
    targets = (
        lax.rem(row + 1, n_row) * n_col + col,
        lax.rem(row + n_row - 1, n_row) * n_col + col,
        row * n_col + lax.rem(col + 1, n_col),
        row * n_col + lax.rem(col + n_col - 1, n_col),
    )

    def ghost_copies(send, recv, send_sem, recv_sem):
        return [
            pltpu.make_async_remote_copy(
                src_ref=send.at[d],
                dst_ref=recv.at[d],
                send_sem=send_sem.at[d],
                recv_sem=recv_sem.at[d],
                device_id=targets[d],
                device_id_type=LOGICAL,
            )
            for d in range(4)
        ]

    head_copies = ghost_copies(hsend, hrecv, hs_sem, hr_sem)
    rest_copies = ghost_copies(gsend, grecv, gs_sem, gr_sem)

    def pack(send, pairs, start, stop):
        picked = nn(ihl[start:stop, :], ones_at(iota((elems, 4 * small), 0) == listed))
        for side in range(2):
            lanes = slice(side * 128, side * 128 + 128)
            for n, pair in enumerate(pairs):
                ends = []
                for q in pair:
                    at = Q_ORDER.index(q) * 128 - start
                    ends.append(picked[at:at + BASIS, lanes] + picked[at + 64:at + 64 + BASIS, lanes])
                first, second = ends
                send[2 * side, n] = jnp.where(half, first, pltpu.roll(second, 64, 1))
                send[2 * side + 1, n] = jnp.where(half, pltpu.roll(first, 64, 1), second)

    def finish(group):
        for p, total in star_block(source, group):
            high, low = split(padded(integ[p] + factor * total))
            block = Q_ORDER.index(p) * 128
            ihl[block:block + 64, :] = high
            ihl[block + 64:block + 128, :] = low

    def stacked_of(p):
        block = Q_ORDER.index(p) * 128
        high = ihl[block:block + 64, :]
        return jnp.concatenate([high, high, ihl[block + 64:block + 128, :]], axis=0)

    finish(GROUPS[0])
    pack(hsend, HEAD_PAIRS, 0, HEAD)
    for copy in head_copies:
        copy.start()
    for p in GROUPS[0]:
        xs[p] = nn(wp[...], stacked_of(p))
    finish(GROUPS[1])
    finish(GROUPS[2])
    pack(gsend, REST_PAIRS, HEAD, 9 * 128)
    for copy in rest_copies:
        copy.start()

    square_e = (elems, elems)
    for j in range(4):
        seen = nbr[j:j + 1, :]
        key = jnp.where(seen < 4 * elems, seen & (elems - 1), -1)
        glb[j] = nn(ihl[...], ones_at(iota(square_e, 0) == key)).astype(BF)

    exchange_wait(2, qsend, qrecv, q_sem, loc_sem.at[0])
    eye_p = eye(128, 128)
    high, low = split(qrecv[...])
    asked = nt(eye_p, high) + nt(eye_p, low)
    slots = 2 * devices
    item = asked[AT_ITEM:AT_ITEM + 1].astype(jnp.int32) - 1
    oht[...] = ones_at(iota((4 * elems, slots), 0) == item)

    inside = (row > 0, row < n_row - 1, col > 0, col < n_col - 1)

    def unpack(copies, recv, pairs):
        for copy in copies:
            copy.wait_recv()
        for side in range(2):
            lanes = slice(side * 128, side * 128 + 128)
            for n, pair in enumerate(pairs):
                first = jnp.where(inside[2 * side], recv[2 * side, n], 0.0)
                second = jnp.where(inside[2 * side + 1], recv[2 * side + 1, n], 0.0)
                halves = [(pair[0], jnp.where(half, first, pltpu.roll(second, 64, 1)))]
                if pair[1] != pair[0]:
                    halves.append((pair[1], jnp.where(half, pltpu.roll(first, 64, 1), second)))
                for quant, value in halves:
                    high, low = split(padded(value))
                    block = Q_ORDER.index(quant) * 128
                    gtab[block:block + 64, lanes] = high
                    gtab[block + 64:block + 128, lanes] = low

    unpack(head_copies, hrecv, HEAD_PAIRS)

    def neighbours(j, start, stop):
        seen = nbr[j:j + 1, :]
        key = jnp.where(seen < 4 * elems, -1, seen & (elems - 1))
        code = 3 * (lax.shift_right_logical(seen, 8) & 3) + ocode[j:j + 1, :]
        got = nn(gtab[start:stop, :], ones_at(iota(square_e, 0) == key)).astype(BF) + glb[j, start:stop, :]
        for block in range(start // 128, stop // 128):
            at = block * 128 - start
            high, low = got[at:at + 64], got[at + 64:at + 128]
            turns = nn(w12[...], jnp.concatenate([high, high, low], axis=0))
            value = turns[0:24]
            for c in range(1, 12):
                value = jnp.where(code == c, turns[24 * c:24 * c + 24], value)
            nvals[j, Q_ORDER[block]] = value

    fvals[...] = jnp.zeros_like(fvals)
    for j in range(4):
        neighbours(j, 0, HEAD)
        lanes = slice(j * elems, (j + 1) * elems)
        x0, x3, x6 = (xs[q, 32 * j:32 * j + 24, :] for q in (0, 3, 6))
        n0, n3, n6 = (nvals[j, q] for q in (0, 3, 6))
        fvals[0:24, lanes] = 0.5 * (x3 + n3) + 0.5 * (x6 - n6)
        fvals[24:48, lanes] = 0.5 * (x0 + n0)

    high, low = split(fvals[...])
    held = nn(high, oht[...]) + nn(low, oht[...])
    slip = friction_solve(
        held[0:FACE],
        held[24:24 + FACE],
        asked[AT_SHEAR:AT_SHEAR + FACE],
        asked[AT_NORMAL:AT_NORMAL + FACE],
        asked[AT_STATE:AT_STATE + FACE],
        asked[AT_SLIP:AT_SLIP + FACE],
    )
    slip = jnp.concatenate([slip, jnp.zeros((64 - FACE, slots), F32)], axis=0)
    slip_high, slip_low = split(slip)
    going = jnp.zeros((devices, 128), F32)
    blank = jnp.zeros((64, slots), BF)
    for k in range(2):
        owner = ones_at(iota((devices, slots), 1) == 2 * iota((devices, slots), 0) + k)
        for part in (slip_high, slip_low):
            going = going + nt(owner, jnp.concatenate([part, blank] if k == 0 else [blank, part], axis=0))
    vsend[...] = going
    exchange_start(1, vsend, vrecv, v_sem, loc_sem.at[1])

    for group in GROUPS:
        for p in group:
            turned[p] = nn(wv[...], stacked_of(p))
            if p not in GROUPS[0]:
                xs[p] = nn(wp[...], stacked_of(p))
    for group in GROUPS:
        for p, total in star_block(turned, group):
            integ[p] = dofs[p * BASIS:(p + 1) * BASIS, :] + 0.25 * total

    def flux_block(j, side, first, read):
        totals = [None] * 3
        for q in range(QUANT):
            value = read(q)
            for i in range(3):
                r = ((j * 2 + side) * QUANT + first + i) * QUANT + q
                term = flux[r:r + 1, :] * value
                totals[i] = term if totals[i] is None else totals[i] + term
        return totals

    loads[2].wait()
    for j in range(4):
        for first in range(0, QUANT, 3):
            for i, total in enumerate(flux_block(j, 0, first, lambda q: xs[q, 32 * j:32 * j + 24, :])):
                comb[first + i, 24 * j:24 * j + 24, :] = total

    unpack(rest_copies, grecv, REST_PAIRS)
    for j in range(4):
        neighbours(j, HEAD, 9 * 128)
    for j in range(4):
        for first in range(0, QUANT, 3):
            for i, total in enumerate(flux_block(j, 1, first, lambda q: nvals[j, q])):
                spot = (first + i, slice(24 * j, 24 * j + 24))
                comb[spot[0], spot[1], :] = comb[spot[0], spot[1], :] + total

    pushed = nt(jnp.concatenate([slip_high[0:32], slip_low[0:32]], axis=0), oht[...])
    pushed = 2.0 * (pushed[0:24] + pushed[32:56])
    for j in range(4):
        spot = slice(24 * j, 24 * j + 24)
        part = pushed[:, j * elems:(j + 1) * elems]
        comb[3, spot, :] = comb[3, spot, :] - part
        comb[6, spot, :] = comb[6, spot, :] + part

    def lifted(value):
        high, low = split(value)
        return nn(wl[...], jnp.concatenate([high, high], axis=0)) + nn(wl[:, 0:96], low)

    for p in range(QUANT):
        result[p * BASIS:(p + 1) * BASIS, :] = integ[p] + 0.25 * lifted(comb[p])
    store = pltpu.make_async_copy(result, out, out_sem.at[0])
    store.start()

    exchange_wait(1, vsend, vrecv, v_sem, loc_sem.at[1])
    high, low = split(vrecv[...])
    both = ones_at(iota(square, 0) == part_row)
    own = nn(nt(eye_p, high).astype(BF), both) + nn(nt(eye_p, low).astype(BF), both)
    slip_out[...] = jnp.where(rank_row == 0, own[0:FACE], own[64:64 + FACE])

    store.wait()
    for copy in head_copies + rest_copies:
        copy.wait_send()
    exchange_end(2, qsend, q_sem)
    exchange_end(1, vsend, v_sem)


def solution(mesh):
    n_row, n_col = mesh.shape["row"], mesh.shape["col"]
    devices = n_row * n_col

    def per_device(dofs, star, flux, kxi, proj, lift, orient, nbr, ocode, slist, fpart, fitem, sh0, nm0, stv, slp):
        elems = dofs.shape[1]
        vmem, anywhere = pl.BlockSpec(memory_space=pltpu.VMEM), pl.BlockSpec(memory_space=pl.ANY)
        table = pltpu.VMEM((devices, 128), F32)
        pair = pltpu.SemaphoreType.DMA((2,))
        four = pltpu.SemaphoreType.DMA((4,))
        return pl.pallas_call(
            lambda *refs: kernel(n_row, n_col, *refs),
            out_shape=(
                jax.ShapeDtypeStruct(dofs.shape, F32),
                jax.ShapeDtypeStruct(slp.shape, F32),
            ),
            in_specs=[anywhere] * 3 + [vmem] * 13,
            out_specs=(anywhere, vmem),
            scratch_shapes=[
                pltpu.VMEM(dofs.shape, F32),
                pltpu.VMEM(star.shape, F32),
                pltpu.VMEM(flux.shape, F32),
                pltpu.VMEM(dofs.shape, F32),
                pltpu.VMEM((3 * BASIS, 192), BF),
                pltpu.VMEM((3 * BASIS, 192), BF),
                pltpu.VMEM((128, 192), BF),
                pltpu.VMEM((288, 192), F32),
                pltpu.VMEM((288, 192), BF),
                pltpu.VMEM((2, 4 * FACE, BASIS), F32),
                pltpu.VMEM((BASIS, 192), BF),
                pltpu.VMEM((2, QUANT, 3 * BASIS, elems), F32),
                pltpu.VMEM((QUANT, BASIS, elems), F32),
                pltpu.VMEM((QUANT * 128, elems), BF),
                pltpu.VMEM((QUANT, 128, elems), F32),
                pltpu.VMEM((4, QUANT * 128, elems), BF),
                pltpu.VMEM((QUANT * 128, elems), BF),
                pltpu.VMEM((4, QUANT, 24, elems), F32),
                pltpu.VMEM((QUANT, 96, elems), F32),
                pltpu.VMEM((64, 4 * elems), F32),
                pltpu.VMEM((4 * elems, 2 * devices), BF),
                pltpu.VMEM((128, 128), F32),
                pltpu.VMEM((4, 3, BASIS, 128), F32),
                pltpu.VMEM((4, 3, BASIS, 128), F32),
                pltpu.VMEM((4, 2, BASIS, 128), F32),
                pltpu.VMEM((4, 2, BASIS, 128), F32),
                pltpu.VMEM((2 * devices, 128), F32),
                pltpu.VMEM((2 * devices, 128), F32),
                table, table,
                four, four, four, four, pair, pair, pair,
                pltpu.SemaphoreType.DMA((3,)),
                pltpu.SemaphoreType.DMA((1,)),
            ],
            compiler_params=pltpu.CompilerParams(collective_id=0, has_side_effects=True),
        )(
            dofs, star, flux, kxi, jnp.transpose(proj, (2, 0, 1)), jnp.transpose(lift, (1, 0, 2)), orient,
            nbr, ocode, slist, fpart.reshape(1, -1), fitem.reshape(1, -1), sh0, nm0, stv, slp,
        )

    split_cols = P(None, ("row", "col"))
    placed = (
        (split_cols,) * 3
        + (P(),) * 4
        + (split_cols,) * 3
        + (P(("row", "col"), None), P(("row", "col")))
        + (split_cols,) * 4
    )
    return jax.shard_map(
        per_device, mesh=mesh, in_specs=placed, out_specs=(split_cols, split_cols), check_vma=False
    )
```

time: 42.1 us -> 33.2 us (0.79)
  Pallas kernels: 38.8 us -> 29.9 us
    pallas_call x1, Pallas kernels: 38.8 us -> 29.9 us  [per_device(): pl.pallas_call(lambda *refs: kernel(n_row, n_col, *refs), out_shape=(jax....]
where the time goes in v2:
time: 33.2 us; the launch traced here: 33 us
  Pallas kernels  29.9 us (90%)
  local copies, waits for them, and re-layouts  2.47 us (7%)
  between operations  0.65 us (2%)
    pallas_call x1, Pallas kernels, per_device(): pl.pallas_call(lambda *refs: kernel(n_row, n_col, *refs), out_shape=(jax....  29.9 us
    unnamed x4, local copies, waits for them, and re-layouts  2.47 us

profile of v2, /device:TPU:1, one launch (start us, length us, event | category | flops | bytes accessed | tf_op | source)
XLA Modules:
  0.0 33.0 jit_solution(9682305384324858356)
XLA Ops:
  0.6 29.9 %shard_map.167 = (f32[504,256]{1,0:T(8,128)}, f32[21,128]{1,0:T(8,128)}) custom-call(f32[504,256]{1,0:T(8,128)} %refs_0_.1, f32[243,256]{1,0:T(8,128)} %refs_1_.1, f32[648,256]{1,0:T(8,128)} %refs_2_.1, f32[3,56,56]{2,1,0:T(8,128)} %refs_3_.1, f32[21,4,56]{2,1,0:T(4,128)} %bitcast.4, f32[21,4,56]{2,1,0:T(4,128)} %bitcast.5, f32[3,21,21]{2,1,0:T(8,128)} %refs_6_.1, ...), custom_call_target="tpu_custom_call" | custom-call | tf_op jit(solution)/shard_map/pallas_call | solution.py:465
  30.5 0.0 copy-start
  30.5 1.9 %copy.20 = f32[504,256]{1,0:T(8,128)} copy(f32[504,256]{1,0:T(8,128)} %get-tuple-element.4) | data formatting | bytes 1032192
  32.4 0.0 copy-done
  32.4 0.6 %copy.21 = f32[21,128]{1,0:T(8,128)} copy(f32[21,128]{1,0:T(8,128)S(1)} %copy-done) | data formatting | bytes 21504
Async XLA Ops:
  30.5 1.9 %copy-start = (f32[21,128]{1,0:T(8,128)S(1)}, f32[21,128]{1,0:T(8,128)}, u32[]{:S(2)}) copy-start(f32[21,128]{1,0:T(8,128)} %get-tuple-element.5) | copy-start | bytes 32260

commit v3 on v2

--- a/solution.py
+++ b/solution.py
@@ -91,10 +91,10 @@
     n_row, n_col,
     dofs_in, star_in, flux_in, kxi, proj, lift, orient, nbr, ocode, slist, fpart, fitem, sh0, nm0, stv, slp,
     out, slip_out,
-    dofs, star, flux, result,
+    dofs, star, flux,
     wk, wv, wp, wo, w12, tall, wl, adv, integ, ihl, xs, glb, gtab, nvals, comb, fvals, oht, params,
     gsend, grecv, hsend, hrecv, qsend, qrecv, vsend, vrecv,
-    gs_sem, gr_sem, hs_sem, hr_sem, q_sem, v_sem, loc_sem, in_sem, out_sem,
+    gs_sem, gr_sem, hs_sem, hr_sem, q_sem, v_sem, loc_sem, in_sem,
 ):
     devices = n_row * n_col
     loads = [
@@ -160,6 +160,119 @@
         back.append(nn(nt(eye_b, high).astype(BF), at_high) + nn(nt(eye_b, low).astype(BF), at_low))
     wk[...] = jnp.concatenate(back, axis=0).astype(BF)
     wv[...] = jnp.concatenate(forth, axis=0).astype(BF)
+    square = (devices, fitem.shape[1])
+    part_row = fpart[...]
+    wide_part = jnp.sum(jnp.where(iota(square, 0) == iota(square, 1), part_row, 0), axis=1, keepdims=True)
+    earlier = (wide_part == part_row) & (iota(square, 0) < iota(square, 1))
+    rank_row = jnp.sum(jnp.where(earlier, 1, 0), axis=0, keepdims=True)
+    tall_square = (2 * devices, fitem.shape[1])
+    slot_of = ones_at(iota(tall_square, 0) == 2 * part_row + rank_row)
+    params[...] = jnp.zeros_like(params)
+    for at, table in ((AT_SHEAR, sh0), (AT_NORMAL, nm0), (AT_STATE, stv), (AT_SLIP, slp)):
+        params[at:at + FACE, :] = table[...]
+    params[AT_ITEM:AT_ITEM + 1, :] = (fitem[...] + 1).astype(F32)
+    high, low = split(params[...])
+    qsend[...] = nt(slot_of, high) + nt(slot_of, low)
+
+    def put(weights, value, target, q):
+        target[q] = nn(weights[...], stacked(padded(value)))
+
+    loads[0].wait()
+    loads[1].wait()
+    for q in Q_ORDER:
+        start = dofs[q * BASIS:(q + 1) * BASIS, :]
+        integ[q] = TIME_STEP * start
+        put(wk, start, adv.at[0], q)
+
+    def star_block(source, group):
+        sides = []
+        for lanes in (slice(0, 128), slice(128, 256)):
+            totals = [None] * 3
+            for q in Q_ORDER:
+                for d in range(3):
+                    value = source[q, d * BASIS:(d + 1) * BASIS, lanes]
+                    for i, p in enumerate(group):
+                        r = (d * QUANT + p) * QUANT + q
+                        term = star[r:r + 1, lanes] * value
+                        totals[i] = term if totals[i] is None else totals[i] + term
+            sides.append(totals)
+        return [(p, jnp.concatenate([left, right], axis=1)) for p, left, right in zip(group, *sides)]
+
+    factor = TIME_STEP
+    for k in range(1, ORDER - 1):
+        if k == 3:
+            pl.semaphore_wait(barrier, devices - 1)
+            exchange_start(2, qsend, qrecv, q_sem, loc_sem.at[0])
+        factor = factor * TIME_STEP / (k + 1)
+        source, target = adv.at[(k - 1) % 2], adv.at[k % 2]
+        for group in GROUPS:
+            for p, total in star_block(source, group):
+                integ[p] = integ[p] + factor * total
+                put(wk, total, target, p)
+    factor = factor * TIME_STEP / ORDER
+    source, turned = adv.at[(ORDER - 2) % 2], adv.at[(ORDER - 1) % 2]
+
+    small = slist.shape[1]
+    elems = dofs.shape[1]
+    spread = ones_at(lax.rem(iota((small, 4 * small), 1), small) == iota((small, 4 * small), 0))
+    listed = nn(slist[...].astype(F32).astype(BF), spread)
+    listed = jnp.sum(
+        jnp.where(iota((4, 4 * small), 1) // small == iota((4, 4 * small), 0), listed, 0.0), axis=0, keepdims=True
+    ).astype(jnp.int32)
+    half = iota((BASIS, 128), 1) < 64
+    targets = (
+        lax.rem(row + 1, n_row) * n_col + col,
+        lax.rem(row + n_row - 1, n_row) * n_col + col,
+        row * n_col + lax.rem(col + 1, n_col),
+        row * n_col + lax.rem(col + n_col - 1, n_col),
+    )
+
+    def ghost_copies(send, recv, send_sem, recv_sem):
+        return [
+            pltpu.make_async_remote_copy(
+                src_ref=send.at[d],
+                dst_ref=recv.at[d],
+                send_sem=send_sem.at[d],
+                recv_sem=recv_sem.at[d],
+                device_id=targets[d],
+                device_id_type=LOGICAL,
+            )
+            for d in range(4)
+        ]
+
+    head_copies = ghost_copies(hsend, hrecv, hs_sem, hr_sem)
+    rest_copies = ghost_copies(gsend, grecv, gs_sem, gr_sem)
+
+    def pack(send, pairs, start, stop):
+        picked = nn(ihl[start:stop, :], ones_at(iota((elems, 4 * small), 0) == listed))
+        for side in range(2):
+            lanes = slice(side * 128, side * 128 + 128)
+            for n, pair in enumerate(pairs):
+                ends = []
+                for q in pair:
+                    at = Q_ORDER.index(q) * 128 - start
+                    ends.append(picked[at:at + BASIS, lanes] + picked[at + 64:at + 64 + BASIS, lanes])
+                first, second = ends
+                send[2 * side, n] = jnp.where(half, first, pltpu.roll(second, 64, 1))
+                send[2 * side + 1, n] = jnp.where(half, pltpu.roll(first, 64, 1), second)
+
+    def finish(group):
+        for p, total in star_block(source, group):
+            high, low = split(padded(integ[p] + factor * total))
+            block = Q_ORDER.index(p) * 128
+            ihl[block:block + 64, :] = high
+            ihl[block + 64:block + 128, :] = low
+
+    def stacked_of(p):
+        block = Q_ORDER.index(p) * 128
+        high = ihl[block:block + 64, :]
+        return jnp.concatenate([high, high, ihl[block + 64:block + 128, :]], axis=0)
+
+    finish(GROUPS[0])
+    pack(hsend, HEAD_PAIRS, 0, HEAD)
+    for copy in head_copies:
+        copy.start()
+
     flat = 4 * FACE
     for g in range(FACE):
         tall[0, 4 * g:4 * g + 4, :] = proj[g]
@@ -182,125 +295,6 @@
         high, low = split(nn(turn, both))
         wo[72 * j:72 * j + 72, :] = nn(high, at_high) + nn(low, at_low)
     w12[...] = wo[...].astype(BF)
-    shape = (flat, 192)
-    spot = 24 * lax.rem(iota(shape, 0), 4) + iota(shape, 0) // 4
-    high, low = split(tall[1])
-    table = nn(nt(eye_b, high).astype(BF), ones_at(iota(shape, 1) == spot))
-    table = table + nn(nt(eye_b, low).astype(BF), ones_at(iota(shape, 1) == spot + 96))
-    wl[...] = table.astype(BF)
-
-    square = (devices, fitem.shape[1])
-    part_row = fpart[...]
-    wide_part = jnp.sum(jnp.where(iota(square, 0) == iota(square, 1), part_row, 0), axis=1, keepdims=True)
-    earlier = (wide_part == part_row) & (iota(square, 0) < iota(square, 1))
-    rank_row = jnp.sum(jnp.where(earlier, 1, 0), axis=0, keepdims=True)
-    tall_square = (2 * devices, fitem.shape[1])
-    slot_of = ones_at(iota(tall_square, 0) == 2 * part_row + rank_row)
-    params[...] = jnp.zeros_like(params)
-    for at, table in ((AT_SHEAR, sh0), (AT_NORMAL, nm0), (AT_STATE, stv), (AT_SLIP, slp)):
-        params[at:at + FACE, :] = table[...]
-    params[AT_ITEM:AT_ITEM + 1, :] = (fitem[...] + 1).astype(F32)
-    high, low = split(params[...])
-    qsend[...] = nt(slot_of, high) + nt(slot_of, low)
-
-    def put(weights, value, target, q):
-        target[q] = nn(weights[...], stacked(padded(value)))
-
-    loads[0].wait()
-    loads[1].wait()
-    for q in Q_ORDER:
-        start = dofs[q * BASIS:(q + 1) * BASIS, :]
-        integ[q] = TIME_STEP * start
-        put(wk, start, adv.at[0], q)
-
-    def star_block(source, group):
-        sides = []
-        for lanes in (slice(0, 128), slice(128, 256)):
-            totals = [None] * 3
-            for q in Q_ORDER:
-                for d in range(3):
-                    value = source[q, d * BASIS:(d + 1) * BASIS, lanes]
-                    for i, p in enumerate(group):
-                        r = (d * QUANT + p) * QUANT + q
-                        term = star[r:r + 1, lanes] * value
-                        totals[i] = term if totals[i] is None else totals[i] + term
-            sides.append(totals)
-        return [(p, jnp.concatenate([left, right], axis=1)) for p, left, right in zip(group, *sides)]
-
-    factor = TIME_STEP
-    for k in range(1, ORDER - 1):
-        if k == 3:
-            pl.semaphore_wait(barrier, devices - 1)
-            exchange_start(2, qsend, qrecv, q_sem, loc_sem.at[0])
-        factor = factor * TIME_STEP / (k + 1)
-        source, target = adv.at[(k - 1) % 2], adv.at[k % 2]
-        for group in GROUPS:
-            for p, total in star_block(source, group):
-                integ[p] = integ[p] + factor * total
-                put(wk, total, target, p)
-    factor = factor * TIME_STEP / ORDER
-    source, turned = adv.at[(ORDER - 2) % 2], adv.at[(ORDER - 1) % 2]
-
-    small = slist.shape[1]
-    elems = dofs.shape[1]
-    spread = ones_at(lax.rem(iota((small, 4 * small), 1), small) == iota((small, 4 * small), 0))
-    listed = nn(slist[...].astype(F32).astype(BF), spread)
-    listed = jnp.sum(
-        jnp.where(iota((4, 4 * small), 1) // small == iota((4, 4 * small), 0), listed, 0.0), axis=0, keepdims=True
-    ).astype(jnp.int32)
-    half = iota((BASIS, 128), 1) < 64
-    targets = (
-        lax.rem(row + 1, n_row) * n_col + col,
-        lax.rem(row + n_row - 1, n_row) * n_col + col,
-        row * n_col + lax.rem(col + 1, n_col),
-        row * n_col + lax.rem(col + n_col - 1, n_col),
-    )
-
-    def ghost_copies(send, recv, send_sem, recv_sem):
-        return [
-            pltpu.make_async_remote_copy(
-                src_ref=send.at[d],
-                dst_ref=recv.at[d],
-                send_sem=send_sem.at[d],
-                recv_sem=recv_sem.at[d],
-                device_id=targets[d],
-                device_id_type=LOGICAL,
-            )
-            for d in range(4)
-        ]
-
-    head_copies = ghost_copies(hsend, hrecv, hs_sem, hr_sem)
-    rest_copies = ghost_copies(gsend, grecv, gs_sem, gr_sem)
-
-    def pack(send, pairs, start, stop):
-        picked = nn(ihl[start:stop, :], ones_at(iota((elems, 4 * small), 0) == listed))
-        for side in range(2):
-            lanes = slice(side * 128, side * 128 + 128)
-            for n, pair in enumerate(pairs):
-                ends = []
-                for q in pair:
-                    at = Q_ORDER.index(q) * 128 - start
-                    ends.append(picked[at:at + BASIS, lanes] + picked[at + 64:at + 64 + BASIS, lanes])
-                first, second = ends
-                send[2 * side, n] = jnp.where(half, first, pltpu.roll(second, 64, 1))
-                send[2 * side + 1, n] = jnp.where(half, pltpu.roll(first, 64, 1), second)
-
-    def finish(group):
-        for p, total in star_block(source, group):
-            high, low = split(padded(integ[p] + factor * total))
-            block = Q_ORDER.index(p) * 128
-            ihl[block:block + 64, :] = high
-            ihl[block + 64:block + 128, :] = low
-
-    def stacked_of(p):
-        block = Q_ORDER.index(p) * 128
-        high = ihl[block:block + 64, :]
-        return jnp.concatenate([high, high, ihl[block + 64:block + 128, :]], axis=0)
-
-    finish(GROUPS[0])
-    pack(hsend, HEAD_PAIRS, 0, HEAD)
-    for copy in head_copies:
-        copy.start()
     for p in GROUPS[0]:
         xs[p] = nn(wp[...], stacked_of(p))
     finish(GROUPS[1])
@@ -388,6 +382,13 @@
     vsend[...] = going
     exchange_start(1, vsend, vrecv, v_sem, loc_sem.at[1])
 
+    shape = (flat, 192)
+    spot = 24 * lax.rem(iota(shape, 0), 4) + iota(shape, 0) // 4
+    high, low = split(tall[1])
+    table = nn(nt(eye_b, high).astype(BF), ones_at(iota(shape, 1) == spot))
+    table = table + nn(nt(eye_b, low).astype(BF), ones_at(iota(shape, 1) == spot + 96))
+    wl[...] = table.astype(BF)
+
     for group in GROUPS:
         for p in group:
             turned[p] = nn(wv[...], stacked_of(p))
@@ -435,9 +436,7 @@
         return nn(wl[...], jnp.concatenate([high, high], axis=0)) + nn(wl[:, 0:96], low)
 
     for p in range(QUANT):
-        result[p * BASIS:(p + 1) * BASIS, :] = integ[p] + 0.25 * lifted(comb[p])
-    store = pltpu.make_async_copy(result, out, out_sem.at[0])
-    store.start()
+        out[p * BASIS:(p + 1) * BASIS, :] = integ[p] + 0.25 * lifted(comb[p])
 
     exchange_wait(1, vsend, vrecv, v_sem, loc_sem.at[1])
     high, low = split(vrecv[...])
@@ -445,11 +444,21 @@
     own = nn(nt(eye_p, high).astype(BF), both) + nn(nt(eye_p, low).astype(BF), both)
     slip_out[...] = jnp.where(rank_row == 0, own[0:FACE], own[64:64 + FACE])
 
-    store.wait()
     for copy in head_copies + rest_copies:
         copy.wait_send()
     exchange_end(2, qsend, q_sem)
     exchange_end(1, vsend, v_sem)
+
+
+def store_results(dofs_ref, slip_ref, dofs_out, slip_out, sem):
+    copies = [
+        pltpu.make_async_copy(source, target, sem.at[n])
+        for n, (source, target) in enumerate(((dofs_ref, dofs_out), (slip_ref, slip_out)))
+    ]
+    for copy in copies:
+        copy.start()
+    for copy in copies:
+        copy.wait()
 
 
 def solution(mesh):
@@ -462,19 +471,15 @@
         table = pltpu.VMEM((devices, 128), F32)
         pair = pltpu.SemaphoreType.DMA((2,))
         four = pltpu.SemaphoreType.DMA((4,))
-        return pl.pallas_call(
+        inside = pl.pallas_call(
             lambda *refs: kernel(n_row, n_col, *refs),
-            out_shape=(
-                jax.ShapeDtypeStruct(dofs.shape, F32),
-                jax.ShapeDtypeStruct(slp.shape, F32),
-            ),
+            out_shape=(pltpu.VMEM(dofs.shape, F32), pltpu.VMEM(slp.shape, F32)),
             in_specs=[anywhere] * 3 + [vmem] * 13,
-            out_specs=(anywhere, vmem),
+            out_specs=(vmem, vmem),
             scratch_shapes=[
                 pltpu.VMEM(dofs.shape, F32),
                 pltpu.VMEM(star.shape, F32),
                 pltpu.VMEM(flux.shape, F32),
-                pltpu.VMEM(dofs.shape, F32),
                 pltpu.VMEM((3 * BASIS, 192), BF),
                 pltpu.VMEM((3 * BASIS, 192), BF),
                 pltpu.VMEM((128, 192), BF),
@@ -502,13 +507,20 @@
                 table, table,
                 four, four, four, four, pair, pair, pair,
                 pltpu.SemaphoreType.DMA((3,)),
-                pltpu.SemaphoreType.DMA((1,)),
             ],
             compiler_params=pltpu.CompilerParams(collective_id=0, has_side_effects=True),
         )(
             dofs, star, flux, kxi, jnp.transpose(proj, (2, 0, 1)), jnp.transpose(lift, (1, 0, 2)), orient,
             nbr, ocode, slist, fpart.reshape(1, -1), fitem.reshape(1, -1), sh0, nm0, stv, slp,
         )
+        return pl.pallas_call(
+            store_results,
+            out_shape=(jax.ShapeDtypeStruct(dofs.shape, F32), jax.ShapeDtypeStruct(slp.shape, F32)),
+            in_specs=[vmem] * 2,
+            out_specs=(anywhere, anywhere),
+            scratch_shapes=[pair],
+            compiler_params=pltpu.CompilerParams(vmem_limit_bytes=1024 * 1024),
+        )(*inside)
 
     split_cols = P(None, ("row", "col"))
     placed = (

time: 33.2 us -> 29.3 us (0.88)
  local copies, waits for them, and re-layouts: 2.47 us -> 0 us
  Pallas kernels: 29.9 us -> 28.3 us
    unnamed x4 -> x0, local copies, waits for them, and re-layouts: 2.47 us -> none
    pallas_call x1 -> x2, Pallas kernels: 29.9 us -> 28.3 us  [the longest x1 27.5 us: per_device(): pl.pallas_call(lambda *refs: kernel(n_row, n_col, *refs), out_shape=(pltp...]
where the time goes in v3:
time: 29.3 us; the launch traced here: 29.2 us
  Pallas kernels  28.3 us (97%)
  between operations  0.81 us (3%)
    pallas_call x1, Pallas kernels, per_device(): pl.pallas_call(lambda *refs: kernel(n_row, n_col, *refs), out_shape=(pltp...  27.5 us
    pallas_call x1, Pallas kernels, per_device(): pl.pallas_call(store_results, out_shape=(jax.ShapeDtypeStruct(dofs.shape,...  0.81 us

profile of v3, /device:TPU:1, one launch (start us, length us, event | category | flops | bytes accessed | tf_op | source)
XLA Modules:
  0.0 29.2 jit_solution(8692216972872965596)
XLA Ops:
  0.6 27.5 %shard_map.167 = (f32[504,256]{1,0:T(8,128)S(1)}, f32[21,128]{1,0:T(8,128)S(1)}) custom-call(f32[504,256]{1,0:T(8,128)} %refs_0_.1, f32[243,256]{1,0:T(8,128)} %refs_1_.1, f32[648,256]{1,0:T(8,128)} %refs_2_.1, f32[3,56,56]{2,1,0:T(8,128)} %refs_3_.1, f32[21,4,56]{2,1,0:T(4,128)} %bitcast.4, f32[21,4,56]{2,1,0:T(4,128)} %bitcast.5, f32[3,21,21]{2,1,0:T(8,128)} %refs_6_.1, ...), custom_call_target="tpu_custom_call" | custom-call | tf_op jit(solution)/shard_map/pallas_call | solution.py:474
  28.2 0.8 %shard_map.168 = (f32[504,256]{1,0:T(8,128)}, f32[21,128]{1,0:T(8,128)}) custom-call(f32[504,256]{1,0:T(8,128)S(1)} %get-tuple-element.4.dofs_ref, f32[21,128]{1,0:T(8,128)S(1)} %get-tuple-element.5.slip_ref), custom_call_target="tpu_custom_call" | custom-call | tf_op jit(solution)/shard_map/pallas_call | solution.py:516

commit v4 on v3

--- a/solution.py
+++ b/solution.py
@@ -17,11 +17,12 @@
 BF = jnp.bfloat16
 F32 = jnp.float32
 
-Q_ORDER = (0, 3, 6, 1, 2, 4, 5, 7, 8)
-GROUPS = (Q_ORDER[0:3], Q_ORDER[3:6], Q_ORDER[6:9])
-HEAD = 3 * 128
-HEAD_PAIRS = ((0, 3), (6, 6))
-REST_PAIRS = ((1, 2), (4, 5), (7, 8))
+DIFF = 9
+BLOCKS = (0, DIFF, 3, 1, 2, 4, 5, 7, 8, 6)
+GROUPS = ((0, 3, 6), (1, 2, 4), (5, 7, 8))
+HEAD, ALL = 2 * 128, 9 * 128
+HEAD_PAIRS = ((0, DIFF),)
+REST_PAIRS = ((3, 1), (2, 4), (5, 7), (8, 8))
 AT_SHEAR, AT_NORMAL, AT_STATE, AT_SLIP, AT_ITEM = 0, 24, 48, 72, 96
 
 
@@ -179,7 +180,7 @@
 
     loads[0].wait()
     loads[1].wait()
-    for q in Q_ORDER:
+    for q in (0, 3, 6, 1, 2, 4, 5, 7, 8):
         start = dofs[q * BASIS:(q + 1) * BASIS, :]
         integ[q] = TIME_STEP * start
         put(wk, start, adv.at[0], q)
@@ -188,7 +189,7 @@
         sides = []
         for lanes in (slice(0, 128), slice(128, 256)):
             totals = [None] * 3
-            for q in Q_ORDER:
+            for q in (0, 3, 6, 1, 2, 4, 5, 7, 8):
                 for d in range(3):
                     value = source[q, d * BASIS:(d + 1) * BASIS, lanes]
                     for i, p in enumerate(group):
@@ -250,21 +251,24 @@
             for n, pair in enumerate(pairs):
                 ends = []
                 for q in pair:
-                    at = Q_ORDER.index(q) * 128 - start
+                    at = BLOCKS.index(q) * 128 - start
                     ends.append(picked[at:at + BASIS, lanes] + picked[at + 64:at + 64 + BASIS, lanes])
                 first, second = ends
                 send[2 * side, n] = jnp.where(half, first, pltpu.roll(second, 64, 1))
                 send[2 * side + 1, n] = jnp.where(half, pltpu.roll(first, 64, 1), second)
 
     def finish(group):
-        for p, total in star_block(source, group):
-            high, low = split(padded(integ[p] + factor * total))
-            block = Q_ORDER.index(p) * 128
+        values = {p: integ[p] + factor * total for p, total in star_block(source, group)}
+        if group == GROUPS[0]:
+            values[DIFF] = values[3] - values[6]
+        for p, value in values.items():
+            high, low = split(padded(value))
+            block = BLOCKS.index(p) * 128
             ihl[block:block + 64, :] = high
             ihl[block + 64:block + 128, :] = low
 
     def stacked_of(p):
-        block = Q_ORDER.index(p) * 128
+        block = BLOCKS.index(p) * 128
         high = ihl[block:block + 64, :]
         return jnp.concatenate([high, high, ihl[block + 64:block + 128, :]], axis=0)
 
@@ -299,7 +303,7 @@
         xs[p] = nn(wp[...], stacked_of(p))
     finish(GROUPS[1])
     finish(GROUPS[2])
-    pack(gsend, REST_PAIRS, HEAD, 9 * 128)
+    pack(gsend, REST_PAIRS, HEAD, ALL)
     for copy in rest_copies:
         copy.start()
 
@@ -307,7 +311,7 @@
     for j in range(4):
         seen = nbr[j:j + 1, :]
         key = jnp.where(seen < 4 * elems, seen & (elems - 1), -1)
-        glb[j] = nn(ihl[...], ones_at(iota(square_e, 0) == key)).astype(BF)
+        glb[j] = nn(ihl[0:ALL, :], ones_at(iota(square_e, 0) == key)).astype(BF)
 
     exchange_wait(2, qsend, qrecv, q_sem, loc_sem.at[0])
     eye_p = eye(128, 128)
@@ -332,7 +336,7 @@
                     halves.append((pair[1], jnp.where(half, pltpu.roll(first, 64, 1), second)))
                 for quant, value in halves:
                     high, low = split(padded(value))
-                    block = Q_ORDER.index(quant) * 128
+                    block = BLOCKS.index(quant) * 128
                     gtab[block:block + 64, lanes] = high
                     gtab[block + 64:block + 128, lanes] = low
 
@@ -350,16 +354,15 @@
             value = turns[0:24]
             for c in range(1, 12):
                 value = jnp.where(code == c, turns[24 * c:24 * c + 24], value)
-            nvals[j, Q_ORDER[block]] = value
+            nvals[j, BLOCKS[block]] = value
 
     fvals[...] = jnp.zeros_like(fvals)
     for j in range(4):
         neighbours(j, 0, HEAD)
         lanes = slice(j * elems, (j + 1) * elems)
         x0, x3, x6 = (xs[q, 32 * j:32 * j + 24, :] for q in (0, 3, 6))
-        n0, n3, n6 = (nvals[j, q] for q in (0, 3, 6))
-        fvals[0:24, lanes] = 0.5 * (x3 + n3) + 0.5 * (x6 - n6)
-        fvals[24:48, lanes] = 0.5 * (x0 + n0)
+        fvals[0:24, lanes] = 0.5 * (x3 + x6) + 0.5 * nvals[j, DIFF]
+        fvals[24:48, lanes] = 0.5 * (x0 + nvals[j, 0])
 
     high, low = split(fvals[...])
     held = nn(high, oht[...]) + nn(low, oht[...])
@@ -416,7 +419,8 @@
 
     unpack(rest_copies, grecv, REST_PAIRS)
     for j in range(4):
-        neighbours(j, HEAD, 9 * 128)
+        neighbours(j, HEAD, ALL)
+        nvals[j, 6] = nvals[j, 3] - nvals[j, DIFF]
     for j in range(4):
         for first in range(0, QUANT, 3):
             for i, total in enumerate(flux_block(j, 1, first, lambda q: nvals[j, q])):
@@ -489,19 +493,19 @@
                 pltpu.VMEM((BASIS, 192), BF),
                 pltpu.VMEM((2, QUANT, 3 * BASIS, elems), F32),
                 pltpu.VMEM((QUANT, BASIS, elems), F32),
-                pltpu.VMEM((QUANT * 128, elems), BF),
+                pltpu.VMEM((len(BLOCKS) * 128, elems), BF),
                 pltpu.VMEM((QUANT, 128, elems), F32),
                 pltpu.VMEM((4, QUANT * 128, elems), BF),
                 pltpu.VMEM((QUANT * 128, elems), BF),
-                pltpu.VMEM((4, QUANT, 24, elems), F32),
+                pltpu.VMEM((4, len(BLOCKS), 24, elems), F32),
                 pltpu.VMEM((QUANT, 96, elems), F32),
                 pltpu.VMEM((64, 4 * elems), F32),
                 pltpu.VMEM((4 * elems, 2 * devices), BF),
                 pltpu.VMEM((128, 128), F32),
-                pltpu.VMEM((4, 3, BASIS, 128), F32),
-                pltpu.VMEM((4, 3, BASIS, 128), F32),
-                pltpu.VMEM((4, 2, BASIS, 128), F32),
-                pltpu.VMEM((4, 2, BASIS, 128), F32),
+                pltpu.VMEM((4, len(REST_PAIRS), BASIS, 128), F32),
+                pltpu.VMEM((4, len(REST_PAIRS), BASIS, 128), F32),
+                pltpu.VMEM((4, len(HEAD_PAIRS), BASIS, 128), F32),
+                pltpu.VMEM((4, len(HEAD_PAIRS), BASIS, 128), F32),
                 pltpu.VMEM((2 * devices, 128), F32),
                 pltpu.VMEM((2 * devices, 128), F32),
                 table, table,

time: 29.3 us -> 28.8 us (0.983)
  Pallas kernels: 28.3 us -> 27.8 us
    pallas_call x1, Pallas kernels: 27.5 us -> 27 us  [per_device(): pl.pallas_call(lambda *refs: kernel(n_row, n_col, *refs), out_shape=(pltp...]
where the time goes in v4:
time: 28.8 us; the launch traced here: 28.6 us
  Pallas kernels  27.8 us (97%)
  between operations  0.81 us (3%)
    pallas_call x1, Pallas kernels, per_device(): pl.pallas_call(lambda *refs: kernel(n_row, n_col, *refs), out_shape=(pltp...  27 us
    pallas_call x1, Pallas kernels, per_device(): pl.pallas_call(store_results, out_shape=(jax.ShapeDtypeStruct(dofs.shape,...  0.81 us

profile of v4, /device:TPU:1, one launch (start us, length us, event | category | flops | bytes accessed | tf_op | source)
XLA Modules:
  0.0 28.6 jit_solution(12171426628529451054)
XLA Ops:
  0.6 27.0 %shard_map.167 = (f32[504,256]{1,0:T(8,128)S(1)}, f32[21,128]{1,0:T(8,128)S(1)}) custom-call(f32[504,256]{1,0:T(8,128)} %refs_0_.1, f32[243,256]{1,0:T(8,128)} %refs_1_.1, f32[648,256]{1,0:T(8,128)} %refs_2_.1, f32[3,56,56]{2,1,0:T(8,128)} %refs_3_.1, f32[21,4,56]{2,1,0:T(4,128)} %bitcast.4, f32[21,4,56]{2,1,0:T(4,128)} %bitcast.5, f32[3,21,21]{2,1,0:T(8,128)} %refs_6_.1, ...), custom_call_target="tpu_custom_call" | custom-call | tf_op jit(solution)/shard_map/pallas_call | solution.py:478
  27.6 0.8 %shard_map.168 = (f32[504,256]{1,0:T(8,128)}, f32[21,128]{1,0:T(8,128)}) custom-call(f32[504,256]{1,0:T(8,128)S(1)} %get-tuple-element.4.dofs_ref, f32[21,128]{1,0:T(8,128)S(1)} %get-tuple-element.5.slip_ref), custom_call_target="tpu_custom_call" | custom-call | tf_op jit(solution)/shard_map/pallas_call | solution.py:520

commit v5 on v4

--- a/solution.py
+++ b/solution.py
@@ -90,9 +90,10 @@
 
 def kernel(
     n_row, n_col,
-    dofs_in, star_in, flux_in, kxi, proj, lift, orient, nbr, ocode, slist, fpart, fitem, sh0, nm0, stv, slp,
+    dofs_in, star_in, flux_in, kxi_in, proj_in, lift_in, orient_in, nbr_in, ocode_in, slist_in, fpart_in, fitem_in,
+    sh0_in, nm0_in, stv_in, slp_in,
     out, slip_out,
-    dofs, star, flux,
+    dofs, star, flux, kxi, proj, lift, orient, nbr, ocode, slist, fpart, fitem, sh0, nm0, stv, slp,
     wk, wv, wp, wo, w12, tall, wl, adv, integ, ihl, xs, glb, gtab, nvals, comb, fvals, oht, params,
     gsend, grecv, hsend, hrecv, qsend, qrecv, vsend, vrecv,
     gs_sem, gr_sem, hs_sem, hr_sem, q_sem, v_sem, loc_sem, in_sem,
@@ -100,9 +101,15 @@
     devices = n_row * n_col
     loads = [
         pltpu.make_async_copy(source, target, in_sem.at[n])
-        for n, (source, target) in enumerate(((dofs_in, dofs), (star_in, star), (flux_in, flux)))
+        for n, (source, target) in enumerate(
+            (
+                (dofs_in, dofs), (star_in, star), (flux_in, flux), (kxi_in, kxi), (proj_in, proj), (lift_in, lift),
+                (orient_in, orient), (nbr_in, nbr), (ocode_in, ocode), (slist_in, slist), (fpart_in, fpart),
+                (fitem_in, fitem), (sh0_in, sh0), (nm0_in, nm0), (stv_in, stv), (slp_in, slp),
+            )
+        )
     ]
-    for load in loads:
+    for load in loads[3:] + loads[0:3]:
         load.start()
     row, col = lax.axis_index("row"), lax.axis_index("col")
     me = row * n_col + col
@@ -151,6 +158,9 @@
     def exchange_end(n, send, sem):
         part = pl.ds(0, n * (devices - 1))
         pltpu.make_async_copy(send.at[part], send.at[part], sem.at[0]).wait()
+
+    for load in loads[3:]:
+        load.wait()
 
     at_high, at_low = place(BASIS, 192, (0, 128)), place(BASIS, 192, (64,))
     eye_b = eye(BASIS, BASIS)
@@ -475,15 +485,17 @@
         table = pltpu.VMEM((devices, 128), F32)
         pair = pltpu.SemaphoreType.DMA((2,))
         four = pltpu.SemaphoreType.DMA((4,))
+        operands = (
+            dofs, star, flux, kxi, jnp.transpose(proj, (2, 0, 1)), jnp.transpose(lift, (1, 0, 2)), orient,
+            nbr, ocode, slist, fpart.reshape(1, -1), fitem.reshape(1, -1), sh0, nm0, stv, slp,
+        )
         inside = pl.pallas_call(
             lambda *refs: kernel(n_row, n_col, *refs),
             out_shape=(pltpu.VMEM(dofs.shape, F32), pltpu.VMEM(slp.shape, F32)),
-            in_specs=[anywhere] * 3 + [vmem] * 13,
+            in_specs=[anywhere] * 16,
             out_specs=(vmem, vmem),
             scratch_shapes=[
-                pltpu.VMEM(dofs.shape, F32),
-                pltpu.VMEM(star.shape, F32),
-                pltpu.VMEM(flux.shape, F32),
+                *(pltpu.VMEM(operand.shape, operand.dtype) for operand in operands),
                 pltpu.VMEM((3 * BASIS, 192), BF),
                 pltpu.VMEM((3 * BASIS, 192), BF),
                 pltpu.VMEM((128, 192), BF),
@@ -510,13 +522,10 @@
                 pltpu.VMEM((2 * devices, 128), F32),
                 table, table,
                 four, four, four, four, pair, pair, pair,
-                pltpu.SemaphoreType.DMA((3,)),
+                pltpu.SemaphoreType.DMA((16,)),
             ],
             compiler_params=pltpu.CompilerParams(collective_id=0, has_side_effects=True),
-        )(
-            dofs, star, flux, kxi, jnp.transpose(proj, (2, 0, 1)), jnp.transpose(lift, (1, 0, 2)), orient,
-            nbr, ocode, slist, fpart.reshape(1, -1), fitem.reshape(1, -1), sh0, nm0, stv, slp,
-        )
+        )(*operands)
         return pl.pallas_call(
             store_results,
             out_shape=(jax.ShapeDtypeStruct(dofs.shape, F32), jax.ShapeDtypeStruct(slp.shape, F32)),

time: 28.8 us -> 27.9 us (0.969)
  Pallas kernels: 27.8 us -> 27 us
    pallas_call x1, Pallas kernels: 27 us -> 26.2 us  [per_device(): pl.pallas_call(lambda *refs: kernel(n_row, n_col, *refs), out_shape=(pltp...]
where the time goes in v5:
time: 27.9 us; the launch traced here: 27.8 us
  Pallas kernels  27 us (97%)
  between operations  0.81 us (3%)
    pallas_call x1, Pallas kernels, per_device(): pl.pallas_call(lambda *refs: kernel(n_row, n_col, *refs), out_shape=(pltp...  26.2 us
    pallas_call x1, Pallas kernels, per_device(): pl.pallas_call(store_results, out_shape=(jax.ShapeDtypeStruct(dofs.shape,...  0.81 us

profile of v5, /device:TPU:1, one launch (start us, length us, event | category | flops | bytes accessed | tf_op | source)
XLA Modules:
  0.0 27.8 jit_solution(2056405485882501670)
XLA Ops:
  0.6 26.2 %shard_map.167 = (f32[504,256]{1,0:T(8,128)S(1)}, f32[21,128]{1,0:T(8,128)S(1)}) custom-call(f32[504,256]{1,0:T(8,128)} %refs_0_.1, f32[243,256]{1,0:T(8,128)} %refs_1_.1, f32[648,256]{1,0:T(8,128)} %refs_2_.1, f32[3,56,56]{2,1,0:T(8,128)} %refs_3_.1, f32[21,4,56]{2,1,0:T(4,128)} %bitcast.4, f32[21,4,56]{2,1,0:T(4,128)} %bitcast.5, f32[3,21,21]{2,1,0:T(8,128)} %refs_6_.1, ...), custom_call_target="tpu_custom_call" | custom-call | tf_op jit(solution)/shard_map/pallas_call | solution.py:492
  26.9 0.8 %shard_map.168 = (f32[504,256]{1,0:T(8,128)}, f32[21,128]{1,0:T(8,128)}) custom-call(f32[504,256]{1,0:T(8,128)S(1)} %get-tuple-element.4.dofs_ref, f32[21,128]{1,0:T(8,128)S(1)} %get-tuple-element.5.slip_ref), custom_call_target="tpu_custom_call" | custom-call | tf_op jit(solution)/shard_map/pallas_call | solution.py:529

commit v6 on v5

--- a/solution.py
+++ b/solution.py
@@ -164,13 +164,35 @@
 
     at_high, at_low = place(BASIS, 192, (0, 128)), place(BASIS, 192, (64,))
     eye_b = eye(BASIS, BASIS)
-    back, forth = [], []
+    back = []
     for d in range(3):
         high, low = split(kxi[d])
-        forth.append(nn(high, at_high) + nn(low, at_low))
         back.append(nn(nt(eye_b, high).astype(BF), at_high) + nn(nt(eye_b, low).astype(BF), at_low))
     wk[...] = jnp.concatenate(back, axis=0).astype(BF)
-    wv[...] = jnp.concatenate(forth, axis=0).astype(BF)
+    def put(weights, value, target, q):
+        target[q] = nn(weights[...], stacked(padded(value)))
+
+    loads[0].wait()
+    loads[1].wait()
+    for q in (0, 3, 6, 1, 2, 4, 5, 7, 8):
+        start = dofs[q * BASIS:(q + 1) * BASIS, :]
+        integ[q] = TIME_STEP * start
+        put(wk, start, adv.at[0], q)
+
+    def star_block(source, group):
+        sides = []
+        for lanes in (slice(0, 128), slice(128, 256)):
+            totals = [None] * 3
+            for q in (0, 3, 6, 1, 2, 4, 5, 7, 8):
+                for d in range(3):
+                    value = source[q, d * BASIS:(d + 1) * BASIS, lanes]
+                    for i, p in enumerate(group):
+                        r = (d * QUANT + p) * QUANT + q
+                        term = star[r:r + 1, lanes] * value
+                        totals[i] = term if totals[i] is None else totals[i] + term
+            sides.append(totals)
+        return [(p, jnp.concatenate([left, right], axis=1)) for p, left, right in zip(group, *sides)]
+
     square = (devices, fitem.shape[1])
     part_row = fpart[...]
     wide_part = jnp.sum(jnp.where(iota(square, 0) == iota(square, 1), part_row, 0), axis=1, keepdims=True)
@@ -184,30 +206,6 @@
     params[AT_ITEM:AT_ITEM + 1, :] = (fitem[...] + 1).astype(F32)
     high, low = split(params[...])
     qsend[...] = nt(slot_of, high) + nt(slot_of, low)
-
-    def put(weights, value, target, q):
-        target[q] = nn(weights[...], stacked(padded(value)))
-
-    loads[0].wait()
-    loads[1].wait()
-    for q in (0, 3, 6, 1, 2, 4, 5, 7, 8):
-        start = dofs[q * BASIS:(q + 1) * BASIS, :]
-        integ[q] = TIME_STEP * start
-        put(wk, start, adv.at[0], q)
-
-    def star_block(source, group):
-        sides = []
-        for lanes in (slice(0, 128), slice(128, 256)):
-            totals = [None] * 3
-            for q in (0, 3, 6, 1, 2, 4, 5, 7, 8):
-                for d in range(3):
-                    value = source[q, d * BASIS:(d + 1) * BASIS, lanes]
-                    for i, p in enumerate(group):
-                        r = (d * QUANT + p) * QUANT + q
-                        term = star[r:r + 1, lanes] * value
-                        totals[i] = term if totals[i] is None else totals[i] + term
-            sides.append(totals)
-        return [(p, jnp.concatenate([left, right], axis=1)) for p, left, right in zip(group, *sides)]
 
     factor = TIME_STEP
     for k in range(1, ORDER - 1):
@@ -287,6 +285,11 @@
     for copy in head_copies:
         copy.start()
 
+    forth = []
+    for d in range(3):
+        high, low = split(kxi[d])
+        forth.append(nn(high, at_high) + nn(low, at_low))
+    wv[...] = jnp.concatenate(forth, axis=0).astype(BF)
     flat = 4 * FACE
     for g in range(FACE):
         tall[0, 4 * g:4 * g + 4, :] = proj[g]

time: 27.9 us -> 27.9 us (level)
  no operation moved by 1% of the time
where the time goes in v6:
time: 27.9 us; the launch traced here: 27.8 us
  Pallas kernels  27 us (97%)
  between operations  0.81 us (3%)
    pallas_call x1, Pallas kernels, per_device(): pl.pallas_call(lambda *refs: kernel(n_row, n_col, *refs), out_shape=(pltp...  26.2 us
    pallas_call x1, Pallas kernels, per_device(): pl.pallas_call(store_results, out_shape=(jax.ShapeDtypeStruct(dofs.shape,...  0.81 us

profile of v6, /device:TPU:1, one launch (start us, length us, event | category | flops | bytes accessed | tf_op | source)
XLA Modules:
  0.0 27.8 jit_solution(17346537967754098623)
XLA Ops:
  0.6 26.2 %shard_map.167 = (f32[504,256]{1,0:T(8,128)S(1)}, f32[21,128]{1,0:T(8,128)S(1)}) custom-call(f32[504,256]{1,0:T(8,128)} %refs_0_.1, f32[243,256]{1,0:T(8,128)} %refs_1_.1, f32[648,256]{1,0:T(8,128)} %refs_2_.1, f32[3,56,56]{2,1,0:T(8,128)} %refs_3_.1, f32[21,4,56]{2,1,0:T(4,128)} %bitcast.4, f32[21,4,56]{2,1,0:T(4,128)} %bitcast.5, f32[3,21,21]{2,1,0:T(8,128)} %refs_6_.1, ...), custom_call_target="tpu_custom_call" | custom-call | tf_op jit(solution)/shard_map/pallas_call | solution.py:495
  26.8 0.8 %shard_map.168 = (f32[504,256]{1,0:T(8,128)}, f32[21,128]{1,0:T(8,128)}) custom-call(f32[504,256]{1,0:T(8,128)S(1)} %get-tuple-element.4.dofs_ref, f32[21,128]{1,0:T(8,128)S(1)} %get-tuple-element.5.slip_ref), custom_call_target="tpu_custom_call" | custom-call | tf_op jit(solution)/shard_map/pallas_call | solution.py:532
